TPU v7x, 32 devices: a whole 2x2x4 slice. The times are simulated.
32 devices in a mesh: groups: 2 (over y), sub: 16 (over z, x, core).
Axes of the slice: x: 2, y: 2, z: 4, core: 2. Of those that a mesh axis runs over, the one named last changes fastest.
Arguments:
- samples: bfloat16 [16896, 512], P(('groups', 'sub')), parts along dimension 0, may hold values from -6 to 6
- channel_order: int32 [512], replicated, may hold values from 0 to 511, each once
- merge_table: int32 [9, 3, 256], replicated, may hold values from 0 to 128, as said below
Outputs:
- spectra: float32 [512, 4096], P(('groups', 'sub')), parts along dimension 0
There are 2 independent parts, one for each index of `groups`. A program takes and returns all parts, laid end to end along the dimension named above; an argument that names none is the same for every part. Nothing has to cross between parts.
Inputs may be any that keep to these rules, and one draw needn't show every extreme that they name: `channel_order`: a permutation of the 512 channels. `merge_table`: for level l, entry j is row d = j % 2**(l-1) of merged subband j // 2**(l-1); with C = max(1, 2**(l-2)) and e = 8, entries 0 and 1 lie in [e * (d // (2 e)), e * (d // (2 e)) + min(C, e)), and entry 2 equals entry 0 or entry 0 plus 1.
All inputs are finite; a program needn't handle non-finite values.
Results may differ from a plain program's by a relative error of at most 0.012.
Values may be sent and summed in bfloat16 or wider, within the bound.
No kernel may reach another device: no remote copies, remote signals or barrier semaphores. Data moves between devices by JAX's collectives and lax.ppermute only.
A program may use at most 64 MiB of HBM per device.

v0:
```python
import functools
import math

import jax
import jax.numpy as jnp
import numpy as np
from jax import lax
from jax.experimental import pallas as pl
from jax.experimental.pallas import tpu as pltpu
from jax.sharding import PartitionSpec as P


LOCAL = 5
CH_DEV = 32
SAMPLES = 8192
LANES = 128


def from_partner(block, axis, apart):
    count = lax.axis_size(axis)
    route = []
    for low in range(count):
        high = low | 1 << apart
        if high != low and high < count:
            route += [(low, high), (high, low)]
    return lax.ppermute(block, axis, route)


def delay_rows(values, shifts, margin):
    moved = values
    for bit_num in range(max(1, margin.bit_length())):
        offset = 2**bit_num
        rolled = jnp.pad(moved[:, offset:], ((0, 0), (0, offset)))
        flagged = shifts >> bit_num & 1 == 1
        flagged = flagged[:, None]
        moved = jnp.where(flagged, rolled, moved)
    return moved


def merge_level(current, entries, child_rows, span_rows, time_axis):
    outputs = jnp.arange(entries.shape[1], dtype=jnp.int32)
    starts = 2 * child_rows * (outputs // span_rows)
    lower_rows = jnp.take(current, starts + entries[0], axis=1 - time_axis)
    upper_rows = jnp.take(current, starts + child_rows + entries[1], axis=1 - time_axis)
    moved_rows = delay_rows(upper_rows, entries[2], child_rows)
    return (lower_rows.astype(jnp.float32) + moved_rows.astype(jnp.float32)).astype(jnp.bfloat16)


def spectrum(delays, channels):
    row_count = delays.shape[0]
    length = delays.shape[1]
    fold_size = length // 128
    first_index = jnp.arange(fold_size, dtype=jnp.int32)
    lane_index = jnp.arange(128, dtype=jnp.int32)
    half_index = jnp.arange(64, dtype=jnp.int32)
    angle_one = (
        2.0
        * math.pi
        / fold_size
        * (first_index[:, None] * first_index[None, :] % fold_size).astype(jnp.float32)
    )
    cos_one = jnp.cos(angle_one).astype(jnp.bfloat16)
    sin_one = jnp.sin(angle_one).astype(jnp.bfloat16)
    angle_two = (
        2.0
        * math.pi
        / length
        * (first_index[:, None] * lane_index[None, :] % length).astype(jnp.float32)
    )
    twist_cos = jnp.cos(angle_two)
    twist_sin = jnp.sin(angle_two)
    angle_three = (
        2.0 * math.pi / 128 * (lane_index[:, None] * half_index[None, :] % 128).astype(jnp.float32)
    )
    cos_three = jnp.cos(angle_three).astype(jnp.bfloat16)
    sin_three = jnp.sin(angle_three).astype(jnp.bfloat16)
    series = delays.reshape(row_count, fold_size, 128)
    first_re = jnp.einsum("kn,rnm->rkm", cos_one, series, preferred_element_type=jnp.float32)
    first_im = -jnp.einsum("kn,rnm->rkm", sin_one, series, preferred_element_type=jnp.float32)
    twisted_re = (first_re * twist_cos + first_im * twist_sin).astype(jnp.bfloat16)
    twisted_im = (first_im * twist_cos - first_re * twist_sin).astype(jnp.bfloat16)
    out_re = jnp.einsum(
        "rkn,nj->rjk", twisted_re, cos_three, preferred_element_type=jnp.float32
    ) + jnp.einsum("rkn,nj->rjk", twisted_im, sin_three, preferred_element_type=jnp.float32)
    out_im = jnp.einsum(
        "rkn,nj->rjk", twisted_im, cos_three, preferred_element_type=jnp.float32
    ) - jnp.einsum("rkn,nj->rjk", twisted_re, sin_three, preferred_element_type=jnp.float32)
    power = (out_re * out_re + out_im * out_im) / (length * channels)
    return power.reshape(row_count, 64 * fold_size)


def owner_plan(samples, channel_order, merge_table):
    owners = lax.axis_size("sub")
    owner_index = lax.axis_index("sub")
    owned_rows = CH_DEV // 2
    quarter = CH_DEV // 4
    window = samples.shape[0]
    channels = samples.shape[1]
    ordered = jnp.take(samples, channel_order, axis=1).T.reshape(owners, CH_DEV, window)
    current = lax.all_to_all(ordered, "sub", split_axis=0, concat_axis=2, tiled=True).reshape(
        CH_DEV, window * owners
    )
    for level_num in range(1, LOCAL + 1):
        entries = lax.dynamic_slice_in_dim(
            merge_table[level_num - 1], owner_index * owned_rows, owned_rows, 1
        )
        current = merge_level(
            current, entries, max(1, 2 ** (level_num - 2)), 2 ** (level_num - 1), 1
        )
    block_index = jnp.zeros((), jnp.int32)
    for bit_num in range(owners.bit_length() - 1):
        level_num = LOCAL + bit_num + 1
        half_bit = owner_index >> bit_num & 1
        block_index = block_index * 2 + half_bit
        span_rows = owned_rows * 2 ** (bit_num + 1)
        child_rows = span_rows // 2
        subband = owner_index >> bit_num + 1
        entries = lax.dynamic_slice_in_dim(
            merge_table[level_num - 1],
            subband * span_rows + owned_rows * block_index,
            owned_rows,
            1,
        )
        kept_rows = lax.dynamic_slice_in_dim(current, half_bit * quarter, quarter, 0)
        sent_rows = lax.dynamic_slice_in_dim(current, (1 - half_bit) * quarter, quarter, 0)
        partner = from_partner(sent_rows, "sub", bit_num)
        row_base = quarter * block_index
        is_low = half_bit == 0
        lower_part = jnp.where(is_low, kept_rows, partner)
        upper_part = jnp.where(is_low, partner, kept_rows)
        lower_rows = jnp.take(lower_part, entries[0] - row_base, axis=0)
        upper_rows = jnp.take(upper_part, entries[1] - row_base, axis=0)
        moved_rows = delay_rows(upper_rows, entries[2], child_rows)
        current = (lower_rows.astype(jnp.float32) + moved_rows.astype(jnp.float32)).astype(
            jnp.bfloat16
        )
    return spectrum(current[:, :SAMPLES], channels)


def reverse_bits(value, bits):
    flipped = 0
    for bit_num in range(bits):
        flipped |= (value >> bit_num & 1) << (bits - 1 - bit_num)
    return flipped


def take_along(values, index, axis):
    along = lax.GatherDimensionNumbers(
        offset_dims=(),
        collapsed_slice_dims=(axis,),
        start_index_map=(axis,),
        operand_batching_dims=(1 - axis,),
        start_indices_batching_dims=(1 - axis,),
    )
    return lax.gather(
        values, index[:, :, None], along, (1, 1), mode=lax.GatherScatterMode.PROMISE_IN_BOUNDS
    )


def tree_kernel(
    owners, margin, samples_ref, order_ref, table_ref, keep_ref, send_ref, raw_ref, first_ref,
    pick_ref, cur_ref, picked_ref, final_ref, turned_ref, sem,
):
    window, channels = samples_ref.shape
    levels, _, dmax = table_ref.shape
    quarter = CH_DEV // 4
    pad = margin // 2
    length = pad + window
    offset = (lax.axis_index("sub") * window) % LANES
    load = pltpu.make_async_copy(samples_ref, raw_ref, sem)
    load.start()

    final_ref[...] = jnp.zeros(final_ref.shape, final_ref.dtype)
    lane = lax.broadcasted_iota(jnp.int32, (8, LANES), 1)
    place = lax.broadcasted_iota(jnp.int32, (channels, LANES), 0)
    for side in range(2):
        for tile in range(dmax // LANES):
            parts = [
                take_along(
                    jnp.broadcast_to(
                        order_ref[:, (2 * tile + part) * LANES : (2 * tile + part + 1) * LANES],
                        (8, LANES),
                    ),
                    (2 * lane + side) & (LANES - 1),
                    1,
                )
                for part in range(2)
            ]
            chosen = jnp.where(lane < LANES // 2, parts[0], parts[1])[:1]
            at = side * dmax + tile * LANES
            first_ref[:, at : at + LANES] = jnp.where(place == chosen, 1.0, 0.0).astype(
                jnp.bfloat16
            )
    place = lax.broadcasted_iota(jnp.int32, (dmax, dmax), 0)
    index = lax.broadcasted_iota(jnp.int32, (1, dmax), 1)
    for level in range(1, levels):
        child = 2 ** (level - 1)
        start = (index >> level) * (2 * child)
        for side in range(2):
            chosen = start + side * child + table_ref[level, side : side + 1, :]
            pick_ref[level - 1, :, side * dmax : (side + 1) * dmax] = jnp.where(
                place == chosen, 1.0, 0.0
            ).astype(jnp.bfloat16)
    load.wait()

    row = lax.broadcasted_iota(jnp.int32, (8, LANES), 0)
    zero = jnp.zeros((8, LANES), jnp.float32)
    begin = pad
    for level in range(levels):
        last = level == levels - 1
        if level:
            picked_ref[begin:length, :] = jnp.dot(
                cur_ref[begin:length, :], pick_ref[level - 1], preferred_element_type=jnp.float32
            )
        else:
            picked_ref[begin:length, :] = jnp.dot(
                raw_ref[...], first_ref[...], preferred_element_type=jnp.float32
            )
        reached = (pad - 2**level) // 16 * 16
        for tile in range(dmax // LANES):
            output = tile * LANES + lane
            steps = (output & (2**level - 1)) // (2 * quarter)
            least = (tile * LANES & (2**level - 1)) // (2 * quarter)
            most = ((tile * LANES + LANES - 1) & (2**level - 1)) // (2 * quarter)
            if 2**level <= LANES:
                least, most = 0, (2**level - 1) // (2 * quarter)
            bits = (most - least).bit_length()
            shift = jnp.broadcast_to(
                table_ref[level, 2:3, tile * LANES : (tile + 1) * LANES], (8, LANES)
            )
            rest = row + shift - steps * quarter
            here = rest < 8
            source = rest & 7
            flags = [((steps - least) >> bit & 1) == 1 for bit in range(bits)]
            known = {}

            def coarse(bit, at):
                if at >= length // 8:
                    return None
                if (bit, at) not in known:
                    if bit == 0:
                        known[bit, at] = (
                            picked_ref[
                                at * 8 : at * 8 + 8,
                                dmax + tile * LANES : dmax + (tile + 1) * LANES,
                            ]
                            if at * 8 >= begin
                            else None
                        )
                    else:
                        near, far = coarse(bit - 1, at), coarse(bit - 1, at + 2 ** (bit - 1))
                        if near is None and far is None:
                            known[bit, at] = None
                        else:
                            near = zero if near is None else near
                            far = zero if far is None else far
                            known[bit, at] = jnp.where(flags[bit - 1], far, near)
                return known[bit, at]

            def fine(at):
                if ("fine", at) not in known:
                    value = coarse(bits, at + least)
                    known["fine", at] = None if value is None else take_along(value, source, 0)
                return known["fine", at]

            def merged(at):
                near, far = fine(at), fine(at + 1)
                total = None
                if near is not None or far is not None:
                    total = jnp.where(
                        here, zero if near is None else near, zero if far is None else far
                    )
                if begin <= at * 8:
                    low = picked_ref[at * 8 : at * 8 + 8, tile * LANES : (tile + 1) * LANES]
                    total = low if total is None else low + total
                return zero if total is None else total

            lanes = slice(tile * LANES, (tile + 1) * LANES)
            for at in range(reached // 8, length // 8, 2):
                both = jnp.concatenate([merged(at), merged(at + 1)], axis=0).astype(jnp.bfloat16)
                if last:
                    to = pl.multiple_of(offset + at * 8 + pad, 16)
                    final_ref[pl.ds(to, 16), lanes] = both
                else:
                    cur_ref[at * 8 : at * 8 + 16, lanes] = both
        begin = max(reached, 0)

    for tile in range(dmax // LANES):
        at = slice(tile * LANES, (tile + 1) * LANES)
        for time in range(final_ref.shape[0] // LANES):
            lanes = slice(time * LANES, (time + 1) * LANES)
            turned_ref[at, lanes] = final_ref[lanes, at].T
    me = lax.axis_index("sub")
    bits = (owners - 1).bit_length()
    rows = dmax // owners
    for ref, core in ((keep_ref, me & 1), (send_ref, 1 - (me & 1))):
        for ring in range(ref.shape[0]):
            for relay in range(2):
                chip, side = (2 * ring + core, core ^ relay) if ring else (relay, core)
                block = reverse_bits(((me >> 1) ^ chip) << 1 | side, bits)
                ref[ring, relay] = turned_ref[pl.ds(pl.multiple_of(block * rows, rows), rows), :]


def pair_kernel(apart, keep_ref, got_ref, own_ref, near_ref, *message_refs):
    lower = lax.axis_index("sub") & 1 == 0
    tiles = keep_ref.shape[-1] // LANES
    for ring in range(keep_ref.shape[0]):
        for relay in range(2):
            for tile in range(apart + tiles):
                total = None
                for start, mine in ((0, lower), (apart, ~lower)):
                    if start <= tile < start + tiles:
                        lanes = slice((tile - start) * LANES, (tile - start + 1) * LANES)
                        part = jnp.where(
                            mine, keep_ref[ring, relay, :, lanes], got_ref[ring, relay, :, lanes]
                        ).astype(jnp.float32)
                        total = part if total is None else total + part
                total = total.astype(own_ref.dtype)
                lanes = slice(tile * LANES, (tile + 1) * LANES)
                if ring:
                    message_refs[ring - 1][relay, :, lanes] = total
                else:
                    (near_ref if relay else own_ref)[:, lanes] = total


def relay_kernel(*refs):
    for at, ref in enumerate(refs[1:-1]):
        refs[-1][at] = ref[1]


def spectrum_kernel(
    rings, scale, own_ref, near_ref, *refs
):
    message_refs, refs = refs[: rings - 1], refs[rings - 1 :]
    relay_ref, first_ref, cos_ref, sin_ref, third_ref, out_ref = refs[:6]
    slot_ref, flat_ref, lines_ref, sems = refs[6:]
    rows, width = own_ref.shape
    tiles = width // LANES
    pitch = slot_ref.shape[0] // rows
    used = first_ref.shape[1]
    bins = first_ref.shape[0] // 2
    halves = third_ref.shape[0] // 2
    me = lax.axis_index("sub")
    core = me & 1
    sources = [(own_ref, (), 0), (near_ref, (), 1)]
    for ring in range(1, rings):
        sources.append((message_refs[ring - 1], (0,), 2 * ring + core))
        sources.append((relay_ref, (ring - 1,), 2 * ring + 1 - core))
    for ref, at, apart in sources:
        slot = ((me >> 1) ^ apart) * tiles
        for tile in range(tiles):
            slot_ref[pl.ds(slot + tile, rows, stride=pitch), :] = ref[
                at + (slice(None), slice(tile * LANES, (tile + 1) * LANES))
            ].astype(jnp.float32)
    lane = lax.broadcasted_iota(jnp.int32, (halves // 2, LANES), 1)
    sign = jnp.where(lax.broadcasted_iota(jnp.int32, (halves, LANES), 1) < bins, 1.0, -1.0)
    stores = []
    for row in range(rows):
        series = slot_ref[row * pitch : row * pitch + used, :].astype(jnp.bfloat16)
        turned = jnp.dot(first_ref[...], series, preferred_element_type=jnp.float32)
        real, imag = turned[:bins], turned[bins:]
        twisted_re = (real * cos_ref[...] - imag * sin_ref[...]).astype(jnp.bfloat16)
        twisted_im = (-imag * cos_ref[...] - real * sin_ref[...]).astype(jnp.bfloat16)
        twisted = jnp.concatenate([twisted_re, twisted_im], axis=0)
        mixed = lax.dot_general(
            third_ref[...], twisted, (((1,), (1,)), ((), ())), preferred_element_type=jnp.float32
        )
        value = mixed[:halves] + sign * pltpu.roll(mixed[halves:], bins, axis=1)
        square = value * value
        power = (square + pltpu.roll(square, bins, axis=1)) * scale
        line = jnp.where(lane < bins, power[: halves // 2], power[halves // 2 :])
        flat_ref[
            pl.ds(row // 8 * 8 * (halves // 2) + row % 8, halves // 2, stride=8), :
        ] = line
        if row % 8 == 7:
            group = row // 8
            for tile in range(halves // 2):
                at = (group * (halves // 2) + tile) * 8
                lines_ref[group * 8 : group * 8 + 8, tile * LANES : (tile + 1) * LANES] = flat_ref[
                    at : at + 8, :
                ]
            stores.append(
                pltpu.make_async_copy(
                    lines_ref.at[pl.ds(group * 8, 8)],
                    out_ref.at[pl.ds(group * 8, 8)],
                    sems.at[group],
                )
            )
            stores[-1].start()
    for store in stores:
        store.wait()


def spectrum_tables(sources, window, margin, tiles):
    fold = SAMPLES // LANES
    k = np.arange(fold)
    n = np.arange(LANES)
    m = np.arange(64)

    def angle(product, period):
        return np.float32(2.0 * math.pi / period) * (product % period).astype(np.float32)

    one = angle(k[:, None] * k[None, :], fold)
    table_one = np.concatenate([np.cos(one), np.sin(one)], axis=0)
    first = np.zeros((2 * fold, sources * tiles), np.float32)
    for source in range(sources):
        start = (source * window) // LANES - margin // LANES
        for tile in range(tiles):
            if 0 <= start + tile < fold:
                first[:, source * tiles + tile] = table_one[:, start + tile]
    two = angle(k[:, None] * n[None, :], SAMPLES)
    m = np.concatenate([m[0::2], m[1::2]])
    three = angle(m[:, None] * n[None, :], LANES)
    third = np.concatenate([np.cos(three), np.sin(three)], axis=0)
    return (
        jnp.asarray(first, jnp.bfloat16),
        jnp.asarray(np.cos(two), jnp.float32),
        jnp.asarray(np.sin(two), jnp.float32),
        jnp.asarray(third, jnp.bfloat16),
    )


def pairs_align(window, owners):
    starts = [at * window // LANES for at in range(owners)]
    return all(starts[at + 1] - starts[at] == window // LANES for at in range(0, owners, 2))


def on_chip(values):
    return pltpu.with_memory_space_constraint(values, pltpu.VMEM)


def slice_plan(samples, channel_order, merge_table):
    owners = lax.axis_size("sub")
    window, channels = samples.shape
    levels, _, dmax = merge_table.shape
    margin = window * owners - SAMPLES
    rows = dmax // owners
    rings = owners // 4
    step = math.gcd(window, LANES)
    width = margin + -(-(window + LANES - step) // LANES) * LANES
    kept = margin // 2 + window
    apart = window // LANES
    wide = width + apart * LANES
    vmem = pl.BlockSpec(memory_space=pltpu.VMEM)
    half = pltpu.VMEM((rings, 2, rows, width), jnp.bfloat16)
    keep, send = pl.pallas_call(
        functools.partial(tree_kernel, owners, margin),
        out_shape=[half, half],
        in_specs=[pl.BlockSpec(memory_space=pl.ANY), vmem, vmem],
        out_specs=[vmem, vmem],
        scratch_shapes=[
            pltpu.VMEM((window, channels), jnp.bfloat16),
            pltpu.VMEM((channels, 2 * dmax), jnp.bfloat16),
            pltpu.VMEM((levels - 1, dmax, 2 * dmax), jnp.bfloat16),
            pltpu.VMEM((kept, dmax), jnp.bfloat16),
            pltpu.VMEM((kept, 2 * dmax), jnp.float32),
            pltpu.VMEM((width, dmax), jnp.bfloat16),
            pltpu.VMEM((dmax, width), jnp.bfloat16),
            pltpu.SemaphoreType.DMA,
        ],
        name="tree",
    )(samples, channel_order.reshape(1, channels), merge_table)
    beside = [(low, low ^ 1) for low in range(owners)]
    got = on_chip(lax.ppermute(send, "sub", beside))
    block = pltpu.VMEM((rows, wide), jnp.bfloat16)
    message = pltpu.VMEM((2, rows, wide), jnp.bfloat16)
    own, near, *messages = pl.pallas_call(
        functools.partial(pair_kernel, apart),
        out_shape=[block, block] + [message] * (rings - 1),
        in_specs=[vmem] * 2,
        out_specs=[vmem] * (rings + 1),
        name="pair",
    )(on_chip(keep), got)
    arrived = []
    for ring in range(rings):
        route = [(a, a ^ (2 * (2 * ring + a % 2) if ring else 2)) for a in range(owners)]
        message = messages[ring - 1] if ring else near
        arrived.append(on_chip(lax.ppermute(message, "sub", route)))
    near, *arrived = arrived
    relay = pl.pallas_call(
        relay_kernel,
        out_shape=pltpu.VMEM((rings - 1, rows, wide), jnp.bfloat16),
        in_specs=[vmem] * rings,
        out_specs=vmem,
        name="relay",
    )(near, *arrived)
    relay = on_chip(lax.ppermute(relay, "sub", beside))
    pairs = owners // 2
    tables = [
        on_chip(table) for table in spectrum_tables(pairs, 2 * window, margin, wide // LANES)
    ]
    pitch = pairs * wide // LANES + 1
    return pl.pallas_call(
        functools.partial(spectrum_kernel, rings, 1.0 / (SAMPLES * channels)),
        out_shape=jax.ShapeDtypeStruct((rows, SAMPLES // 2), jnp.float32),
        in_specs=[vmem] * (rings + 6),
        out_specs=pl.BlockSpec(memory_space=pl.ANY),
        scratch_shapes=[
            pltpu.VMEM((rows * pitch, LANES), jnp.float32),
            pltpu.VMEM((rows * SAMPLES // 2 // LANES, LANES), jnp.float32),
            pltpu.VMEM((rows, SAMPLES // 2), jnp.float32),
            pltpu.SemaphoreType.DMA((rows // 8,)),
        ],
        name="spectrum",
    )(on_chip(own), near, *arrived, relay, *tables)


def local(samples, channel_order, merge_table):
    owners = lax.axis_size("sub")
    window, channels = samples.shape
    dmax = merge_table.shape[2]
    margin = window * owners - SAMPLES
    fits = (
        dmax == 256
        and channels == 2 * dmax
        and dmax == 16 * owners
        and margin == dmax
        and window % 16 == 0
        and window <= 1024
        and owners % 8 == 0
        and pairs_align(window, owners)
    )
    plan = slice_plan if fits else owner_plan
    return plan(samples, channel_order, merge_table)


def solution(mesh):
    in_specs = (P(("groups", "sub"), None), P(), P())
    out_specs = P(("groups", "sub"), None)
    return jax.shard_map(local, mesh=mesh, in_specs=in_specs, out_specs=out_specs, check_vma=False)
```

profile of v0, /device:TPU:0, one launch (start us, length us, event | category | flops | bytes accessed | tf_op | source)
XLA Modules:
  0.0 22.9 jit_solution(6733513171736208715)
XLA Ops:
  0.0 3.8 %tree.1 = (bf16[4,2,16,896]{3,2,1,0:T(8,128)(2,1)S(1)}, bf16[4,2,16,896]{3,2,1,0:T(8,128)(2,1)S(1)}) custom-call(bf16[528,512]{1,0:T(8,128)(2,1)} %samples_ref.1, s32[1,512]{1,0:T(1,128)} %bitcast.1, s32[9,3,256]{2,1,0:T(4,128)} %table_ref.1), custom_call_target="tpu_custom_call" | custom-call | tf_op jit(solution)/shard_map/tree/pallas_call | solution.py:446
  3.8 0.6 %collective-permute-start = (bf16[4,2,16,896]{3,2,1,0:T(8,128)(2,1)S(1)}, bf16[4,2,16,896]{3,2,1,0:T(8,128)(2,1)S(1)}, u32[]{:S(2)}, u32[]{:S(2)}) collective-permute-start(bf16[4,2,16,896]{3,2,1,0:T(8,128)(2,1)S(1)} %get-tuple-element.13), channel_id=1, source_target_pairs={{0,1},{1,0},{2,3},{3,2},{4,5},{5,4},{6,7},{7,6},{8,9},{9,8},{10,11... | collective-permute-start | bytes 688136 | tf_op jit(solution)/shard_map/ppermute | solution.py:464
  4.3 1.1 %collective-permute-done.got_ref = bf16[4,2,16,896]{3,2,1,0:T(8,128)(2,1)S(1)} collective-permute-done((bf16[4,2,16,896]{3,2,1,0:T(8,128)(2,1)S(1)}, bf16[4,2,16,896]{3,2,1,0:T(8,128)(2,1)S(1)}, u32[]{:S(2)}, u32[]{:S(2)}) %collective-permute-start) | collective-permute-done | bytes 229408 | tf_op jit(solution)/shard_map/ppermute | solution.py:464
  5.4 0.1 pair.1
  5.5 3.0 %collective-permute-start.2 = (bf16[2,16,1408]{2,1,0:T(8,128)(2,1)S(1)}, bf16[2,16,1408]{2,1,0:T(8,128)(2,1)S(1)}, u32[]{:S(2)}, u32[]{:S(2)}) collective-permute-start(bf16[2,16,1408]{2,1,0:T(8,128)(2,1)S(1)} %get-tuple-element.16), channel_id=1, source_target_pairs={{0,4},{1,7},{2,6},{3,5},{4,0},{5,3},{6,2},{7,1},{8,12},{9,15},{10,... | collective-permute-start | bytes 270344 | tf_op jit(solution)/shard_map/ppermute | solution.py:478
  8.5 2.6 %collective-permute-start.3 = (bf16[2,16,1408]{2,1,0:T(8,128)(2,1)S(1)}, bf16[2,16,1408]{2,1,0:T(8,128)(2,1)S(1)}, u32[]{:S(2)}, u32[]{:S(2)}) collective-permute-start(bf16[2,16,1408]{2,1,0:T(8,128)(2,1)S(1)} %get-tuple-element.17), channel_id=1, source_target_pairs={{0,8},{1,11},{2,10},{3,9},{4,12},{5,15},{6,14},{7,13},{8,0},{9,3},... | collective-permute-start | bytes 270344 | tf_op jit(solution)/shard_map/ppermute | solution.py:478
  11.1 0.0 collective-permute-start.4
  11.1 0.0 copy-start
  11.1 0.0 copy-start.1
  11.1 0.0 copy-start.2
  11.1 0.0 copy-start.3
  11.1 1.8 %collective-permute-start.1 = (bf16[16,1408]{1,0:T(8,128)(2,1)S(1)}, bf16[16,1408]{1,0:T(8,128)(2,1)S(1)}, u32[]{:S(2)}, u32[]{:S(2)}) collective-permute-start(bf16[16,1408]{1,0:T(8,128)(2,1)S(1)} %get-tuple-element.15), channel_id=1, source_target_pairs={{0,2},{1,3},{2,0},{3,1},{4,6},{5,7},{6,4},{7,5},{8,10},{9,11},{10,... | collective-permute-start | bytes 135176 | tf_op jit(solution)/shard_map/ppermute | solution.py:478
  12.9 2.8 %collective-permute-done.1.refs_0_.near_ref = bf16[16,1408]{1,0:T(8,128)(2,1)S(1)} collective-permute-done((bf16[16,1408]{1,0:T(8,128)(2,1)S(1)}, bf16[16,1408]{1,0:T(8,128)(2,1)S(1)}, u32[]{:S(2)}, u32[]{:S(2)}) %collective-permute-start.1) | collective-permute-done | bytes 45088 | tf_op jit(solution)/shard_map/ppermute | solution.py:478
  15.7 0.0 collective-permute-done.2.refs_1_.refs_0_
  15.7 3.0 %collective-permute-done.3.refs_2_.refs_1_ = bf16[2,16,1408]{2,1,0:T(8,128)(2,1)S(1)} collective-permute-done((bf16[2,16,1408]{2,1,0:T(8,128)(2,1)S(1)}, bf16[2,16,1408]{2,1,0:T(8,128)(2,1)S(1)}, u32[]{:S(2)}, u32[]{:S(2)}) %collective-permute-start.3) | collective-permute-done | bytes 90144 | tf_op jit(solution)/shard_map/ppermute | solution.py:478
  18.7 0.0 collective-permute-done.4.refs_3_.refs_2_
  18.7 0.5 %collective-permute-start.5 = (bf16[3,16,1408]{2,1,0:T(8,128)(2,1)S(1)}, bf16[3,16,1408]{2,1,0:T(8,128)(2,1)S(1)}, u32[]{:S(2)}, u32[]{:S(2)}) collective-permute-start(bf16[3,16,1408]{2,1,0:T(8,128)(2,1)S(1)} %relay.1), channel_id=1, source_target_pairs={{0,1},{1,0},{2,3},{3,2},{4,5},{5,4},{6,7},{7,6},{8,9},{9,8},{10,11... | collective-permute-start | bytes 405512 | tf_op jit(solution)/shard_map/ppermute | solution.py:487
  19.3 1.0 %collective-permute-done.5.refs_3_ = bf16[3,16,1408]{2,1,0:T(8,128)(2,1)S(1)} collective-permute-done((bf16[3,16,1408]{2,1,0:T(8,128)(2,1)S(1)}, bf16[3,16,1408]{2,1,0:T(8,128)(2,1)S(1)}, u32[]{:S(2)}, u32[]{:S(2)}) %collective-permute-start.5) | collective-permute-done | bytes 135200 | tf_op jit(solution)/shard_map/ppermute | solution.py:487
  20.3 0.0 copy-done
  20.3 0.0 copy-done.1
  20.3 0.0 copy-done.2
  20.3 0.0 copy-done.3
  20.3 2.6 %spectrum.1 = f32[16,4096]{1,0:T(8,128)} custom-call(bf16[16,1408]{1,0:T(8,128)(2,1)S(1)} %get-tuple-element.14.own_ref, bf16[16,1408]{1,0:T(8,128)(2,1)S(1)} %collective-permute-done.1.refs_0_.near_ref, bf16[2,16,1408]{2,1,0:T(8,128)(2,1)S(1)} %collective-permute-done.2.refs_1_.refs_0_, bf16[2,16,1408]{2,1,0:T(8,128)(2,1)S(1)} %collective-permute-done.3.refs_2_.refs_1_, ...), custom_call_target="tpu_custom_call" | custom-call | tf_op jit(solution)/shard_map/spectrum/pallas_call | solution.py:493
  (1 shorter events, 0.0 us)
Async XLA Ops:
  3.8 1.7 %collective-permute-start = (bf16[4,2,16,896]{3,2,1,0:T(8,128)(2,1)S(1)}, bf16[4,2,16,896]{3,2,1,0:T(8,128)(2,1)S(1)}, u32[]{:S(2)}, u32[]{:S(2)}) collective-permute-start(bf16[4,2,16,896]{3,2,1,0:T(8,128)(2,1)S(1)} %get-tuple-element.13), channel_id=1, source_target_pairs={{0,1},{1,0},{2,3},{3,2},{4,5},{5,4},{6,7},{7,6},{8,9},{9,8},{10,11... | collective-permute-start | bytes 688136 | tf_op jit(solution)/shard_map/ppermute | solution.py:464
  5.5 10.2 %collective-permute-start.2 = (bf16[2,16,1408]{2,1,0:T(8,128)(2,1)S(1)}, bf16[2,16,1408]{2,1,0:T(8,128)(2,1)S(1)}, u32[]{:S(2)}, u32[]{:S(2)}) collective-permute-start(bf16[2,16,1408]{2,1,0:T(8,128)(2,1)S(1)} %get-tuple-element.16), channel_id=1, source_target_pairs={{0,4},{1,7},{2,6},{3,5},{4,0},{5,3},{6,2},{7,1},{8,12},{9,15},{10,... | collective-permute-start | bytes 270344 | tf_op jit(solution)/shard_map/ppermute | solution.py:478
  8.5 10.2 %collective-permute-start.3 = (bf16[2,16,1408]{2,1,0:T(8,128)(2,1)S(1)}, bf16[2,16,1408]{2,1,0:T(8,128)(2,1)S(1)}, u32[]{:S(2)}, u32[]{:S(2)}) collective-permute-start(bf16[2,16,1408]{2,1,0:T(8,128)(2,1)S(1)} %get-tuple-element.17), channel_id=1, source_target_pairs={{0,8},{1,11},{2,10},{3,9},{4,12},{5,15},{6,14},{7,13},{8,0},{9,3},... | collective-permute-start | bytes 270344 | tf_op jit(solution)/shard_map/ppermute | solution.py:478
  11.1 7.6 %collective-permute-start.4 = (bf16[2,16,1408]{2,1,0:T(8,128)(2,1)S(1)}, bf16[2,16,1408]{2,1,0:T(8,128)(2,1)S(1)}, u32[]{:S(2)}, u32[]{:S(2)}) collective-permute-start(bf16[2,16,1408]{2,1,0:T(8,128)(2,1)S(1)} %get-tuple-element.18), channel_id=1, source_target_pairs={{0,12},{1,15},{2,14},{3,13},{4,8},{5,11},{6,10},{7,9},{8,4},{9,7},... | collective-permute-start | bytes 270344 | tf_op jit(solution)/shard_map/ppermute | solution.py:478
  11.1 9.2 %copy-start = (bf16[128,128]{1,0:T(8,128)(2,1)S(1)}, bf16[128,128]{1,0:T(8,128)(2,1)}, u32[]{:S(2)}) copy-start(bf16[128,128]{1,0:T(8,128)(2,1)} %constant.11.clone.refs_7_) | copy-start | bytes 98308
  11.1 9.2 %copy-start.1 = (f32[64,128]{1,0:T(8,128)S(1)}, f32[64,128]{1,0:T(8,128)}, u32[]{:S(2)}) copy-start(f32[64,128]{1,0:T(8,128)} %constant.10.clone.refs_6_) | copy-start | bytes 98308
  11.1 9.2 %copy-start.2 = (f32[64,128]{1,0:T(8,128)S(1)}, f32[64,128]{1,0:T(8,128)}, u32[]{:S(2)}) copy-start(f32[64,128]{1,0:T(8,128)} %constant.9.clone.refs_5_) | copy-start | bytes 98308
  11.1 9.1 %copy-start.3 = (bf16[128,88]{1,0:T(8,128)(2,1)S(1)}, bf16[128,88]{1,0:T(8,128)(2,1)}, u32[]{:S(2)}) copy-start(bf16[128,88]{1,0:T(8,128)(2,1)} %constant.8.clone.refs_4_) | copy-start | bytes 67588
  11.1 4.5 %collective-permute-start.1 = (bf16[16,1408]{1,0:T(8,128)(2,1)S(1)}, bf16[16,1408]{1,0:T(8,128)(2,1)S(1)}, u32[]{:S(2)}, u32[]{:S(2)}) collective-permute-start(bf16[16,1408]{1,0:T(8,128)(2,1)S(1)} %get-tuple-element.15), channel_id=1, source_target_pairs={{0,2},{1,3},{2,0},{3,1},{4,6},{5,7},{6,4},{7,5},{8,10},{9,11},{10,... | collective-permute-start | bytes 135176 | tf_op jit(solution)/shard_map/ppermute | solution.py:478
  18.7 1.5 %collective-permute-start.5 = (bf16[3,16,1408]{2,1,0:T(8,128)(2,1)S(1)}, bf16[3,16,1408]{2,1,0:T(8,128)(2,1)S(1)}, u32[]{:S(2)}, u32[]{:S(2)}) collective-permute-start(bf16[3,16,1408]{2,1,0:T(8,128)(2,1)S(1)} %relay.1), channel_id=1, source_target_pairs={{0,1},{1,0},{2,3},{3,2},{4,5},{5,4},{6,7},{7,6},{8,9},{9,8},{10,11... | collective-permute-start | bytes 405512 | tf_op jit(solution)/shard_map/ppermute | solution.py:487
where the time goes:
time: 23.1 us; the launch traced here: 22.9 us
  starting transfers between devices  8.45 us (37%)
  waiting for transfers between devices  7.92 us (34%)
  Pallas kernels  6.44 us (28%)
    ppermute x4, starting transfers between devices, slice_plan(): arrived.append(on_chip(lax.ppermute(message, 'sub', route)))  7.35 us
    ppermute x4, waiting for transfers between devices, slice_plan(): arrived.append(on_chip(lax.ppermute(message, 'sub', route)))  5.81 us
    pallas_call x1, Pallas kernels, slice_plan(): pl.pallas_call(functools.partial(tree_kernel, owners, margin), out_shape=...  3.75 us
    pallas_call x1, Pallas kernels, slice_plan(): pl.pallas_call(functools.partial(spectrum_kernel, rings, 1.0 / (SAMPLES *...  2.59 us
    ppermute x1, waiting for transfers between devices, slice_plan(): got = on_chip(lax.ppermute(send, 'sub', beside))  1.12 us
    ppermute x1, waiting for transfers between devices, slice_plan(): relay = on_chip(lax.ppermute(relay, 'sub', beside))  0.99 us
    ppermute x1, starting transfers between devices, slice_plan(): got = on_chip(lax.ppermute(send, 'sub', beside))  0.56 us
    ppermute x1, starting transfers between devices, slice_plan(): relay = on_chip(lax.ppermute(relay, 'sub', beside))  0.54 us
  transfers between devices with their start and end apart: 6, of which 4 were waited for; matrix products, arithmetic and copies ran while one was open for 0% of the time, Pallas kernels for 0%

commit v1 on v0

--- a/solution.py
+++ b/solution.py
@@ -158,21 +158,40 @@
 
 
 def tree_kernel(
-    owners, margin, samples_ref, order_ref, table_ref, keep_ref, send_ref, raw_ref, first_ref,
-    pick_ref, cur_ref, picked_ref, final_ref, turned_ref, sem,
+    owners, margin, samples_at, order_at, table_at, keep_ref, send_ref, raw_ref, order_ref,
+    table_ref, first_ref, pick_ref, cur_ref, picked_ref, final_ref, turned_ref, sems,
 ):
-    window, channels = samples_ref.shape
+    window, channels = raw_ref.shape
     levels, _, dmax = table_ref.shape
     quarter = CH_DEV // 4
     pad = margin // 2
     length = pad + window
     offset = (lax.axis_index("sub") * window) % LANES
-    load = pltpu.make_async_copy(samples_ref, raw_ref, sem)
-    load.start()
+    loads = [
+        pltpu.make_async_copy(source, target, sems.at[at])
+        for at, (source, target) in enumerate(
+            ((table_at, table_ref), (order_at, order_ref), (samples_at, raw_ref))
+        )
+    ]
+    for load in loads:
+        load.start()
 
     final_ref[...] = jnp.zeros(final_ref.shape, final_ref.dtype)
     lane = lax.broadcasted_iota(jnp.int32, (8, LANES), 1)
-    place = lax.broadcasted_iota(jnp.int32, (channels, LANES), 0)
+
+    def narrow(numbers):
+        return numbers.astype(jnp.float32).astype(jnp.bfloat16)
+
+    def one_hot(place, chosen):
+        return jnp.where(
+            place == jnp.broadcast_to(narrow(chosen), place.shape),
+            jnp.ones(place.shape, jnp.bfloat16),
+            jnp.zeros(place.shape, jnp.bfloat16),
+        )
+
+    loads[0].wait()
+    loads[1].wait()
+    place = narrow(lax.broadcasted_iota(jnp.int32, (dmax, LANES), 0))
     for side in range(2):
         for tile in range(dmax // LANES):
             parts = [
@@ -188,20 +207,25 @@
             ]
             chosen = jnp.where(lane < LANES // 2, parts[0], parts[1])[:1]
             at = side * dmax + tile * LANES
-            first_ref[:, at : at + LANES] = jnp.where(place == chosen, 1.0, 0.0).astype(
-                jnp.bfloat16
-            )
-    place = lax.broadcasted_iota(jnp.int32, (dmax, dmax), 0)
+            for part in range(channels // dmax):
+                first_ref[part * dmax : (part + 1) * dmax, at : at + LANES] = one_hot(
+                    place, chosen - part * dmax
+                )
     index = lax.broadcasted_iota(jnp.int32, (1, dmax), 1)
+    place = narrow(lax.broadcasted_iota(jnp.int32, (dmax // 2, LANES), 0))
     for level in range(1, levels):
         child = 2 ** (level - 1)
         start = (index >> level) * (2 * child)
         for side in range(2):
-            chosen = start + side * child + table_ref[level, side : side + 1, :]
-            pick_ref[level - 1, :, side * dmax : (side + 1) * dmax] = jnp.where(
-                place == chosen, 1.0, 0.0
-            ).astype(jnp.bfloat16)
-    load.wait()
+            chosen = (start + side * child + table_ref[level, side : side + 1, :]) & (
+                dmax // 2 - 1
+            )
+            for tile in range(dmax // LANES):
+                part, to = (side, tile) if level == levels - 1 else (tile, side)
+                pick_ref[level - 1, part, :, to * LANES : (to + 1) * LANES] = one_hot(
+                    place, chosen[:, tile * LANES : (tile + 1) * LANES]
+                )
+    loads[2].wait()
 
     row = lax.broadcasted_iota(jnp.int32, (8, LANES), 0)
     zero = jnp.zeros((8, LANES), jnp.float32)
@@ -209,15 +233,22 @@
     for level in range(levels):
         last = level == levels - 1
         if level:
-            picked_ref[begin:length, :] = jnp.dot(
-                cur_ref[begin:length, :], pick_ref[level - 1], preferred_element_type=jnp.float32
-            )
+            for part in range(2):
+                picked_ref[begin:length, part * dmax : (part + 1) * dmax] = jnp.dot(
+                    cur_ref[begin:length, part * LANES : (part + 1) * LANES],
+                    pick_ref[level - 1, part],
+                    preferred_element_type=jnp.float32,
+                )
         else:
             picked_ref[begin:length, :] = jnp.dot(
                 raw_ref[...], first_ref[...], preferred_element_type=jnp.float32
             )
         reached = (pad - 2**level) // 16 * 16
         for tile in range(dmax // LANES):
+            low_at = tile if last or not level else 2 * tile
+            high_at = low_at + (2 if last or not level else 1)
+            low_lanes = slice(low_at * LANES, (low_at + 1) * LANES)
+            high_lanes = slice(high_at * LANES, (high_at + 1) * LANES)
             output = tile * LANES + lane
             steps = (output & (2**level - 1)) // (2 * quarter)
             least = (tile * LANES & (2**level - 1)) // (2 * quarter)
@@ -240,10 +271,7 @@
                 if (bit, at) not in known:
                     if bit == 0:
                         known[bit, at] = (
-                            picked_ref[
-                                at * 8 : at * 8 + 8,
-                                dmax + tile * LANES : dmax + (tile + 1) * LANES,
-                            ]
+                            picked_ref[at * 8 : at * 8 + 8, high_lanes]
                             if at * 8 >= begin
                             else None
                         )
@@ -271,7 +299,7 @@
                         here, zero if near is None else near, zero if far is None else far
                     )
                 if begin <= at * 8:
-                    low = picked_ref[at * 8 : at * 8 + 8, tile * LANES : (tile + 1) * LANES]
+                    low = picked_ref[at * 8 : at * 8 + 8, low_lanes]
                     total = low if total is None else low + total
                 return zero if total is None else total
 
@@ -446,17 +474,19 @@
     keep, send = pl.pallas_call(
         functools.partial(tree_kernel, owners, margin),
         out_shape=[half, half],
-        in_specs=[pl.BlockSpec(memory_space=pl.ANY), vmem, vmem],
+        in_specs=[pl.BlockSpec(memory_space=pl.ANY)] * 3,
         out_specs=[vmem, vmem],
         scratch_shapes=[
             pltpu.VMEM((window, channels), jnp.bfloat16),
+            pltpu.VMEM((1, channels), jnp.int32),
+            pltpu.VMEM((levels, 3, dmax), jnp.int32),
             pltpu.VMEM((channels, 2 * dmax), jnp.bfloat16),
-            pltpu.VMEM((levels - 1, dmax, 2 * dmax), jnp.bfloat16),
+            pltpu.VMEM((levels - 1, 2, dmax // 2, dmax), jnp.bfloat16),
             pltpu.VMEM((kept, dmax), jnp.bfloat16),
             pltpu.VMEM((kept, 2 * dmax), jnp.float32),
             pltpu.VMEM((width, dmax), jnp.bfloat16),
             pltpu.VMEM((dmax, width), jnp.bfloat16),
-            pltpu.SemaphoreType.DMA,
+            pltpu.SemaphoreType.DMA((3,)),
         ],
         name="tree",
     )(samples, channel_order.reshape(1, channels), merge_table)

time: 23.1 us -> 22.3 us (0.965)
  Pallas kernels: 6.44 us -> 5.72 us
    pallas_call x1, Pallas kernels: 3.75 us -> 3.03 us  [slice_plan(): pl.pallas_call(functools.partial(tree_kernel, owners, margin), out_shape=...]
where the time goes in v1:
time: 22.3 us; the launch traced here: 22.1 us
  starting transfers between devices  8.46 us (38%)
  waiting for transfers between devices  7.9 us (35%)
  Pallas kernels  5.72 us (26%)
    ppermute x4, starting transfers between devices, slice_plan(): arrived.append(on_chip(lax.ppermute(message, 'sub', route)))  7.35 us
    ppermute x4, waiting for transfers between devices, slice_plan(): arrived.append(on_chip(lax.ppermute(message, 'sub', route)))  5.8 us
    pallas_call x1, Pallas kernels, slice_plan(): pl.pallas_call(functools.partial(tree_kernel, owners, margin), out_shape=...  3.03 us
    pallas_call x1, Pallas kernels, slice_plan(): pl.pallas_call(functools.partial(spectrum_kernel, rings, 1.0 / (SAMPLES *...  2.59 us
    ppermute x1, waiting for transfers between devices, slice_plan(): got = on_chip(lax.ppermute(send, 'sub', beside))  1.12 us
    ppermute x1, waiting for transfers between devices, slice_plan(): relay = on_chip(lax.ppermute(relay, 'sub', beside))  0.99 us
    ppermute x1, starting transfers between devices, slice_plan(): got = on_chip(lax.ppermute(send, 'sub', beside))  0.56 us
    ppermute x1, starting transfers between devices, slice_plan(): relay = on_chip(lax.ppermute(relay, 'sub', beside))  0.55 us
  transfers between devices with their start and end apart: 6, of which 4 were waited for; matrix products, arithmetic and copies ran while one was open for 0% of the time, Pallas kernels for 0%

profile of v1, /device:TPU:0, one launch (start us, length us, event | category | flops | bytes accessed | tf_op | source)
XLA Modules:
  0.0 22.1 jit_solution(7540397563752577897)
XLA Ops:
  0.0 3.0 %tree.1 = (bf16[4,2,16,896]{3,2,1,0:T(8,128)(2,1)S(1)}, bf16[4,2,16,896]{3,2,1,0:T(8,128)(2,1)S(1)}) custom-call(bf16[528,512]{1,0:T(8,128)(2,1)} %samples_at.1, s32[1,512]{1,0:T(1,128)} %bitcast.1, s32[9,3,256]{2,1,0:T(4,128)} %table_at.1), custom_call_target="tpu_custom_call" | custom-call | tf_op jit(solution)/shard_map/tree/pallas_call | solution.py:474
  3.0 0.6 %collective-permute-start = (bf16[4,2,16,896]{3,2,1,0:T(8,128)(2,1)S(1)}, bf16[4,2,16,896]{3,2,1,0:T(8,128)(2,1)S(1)}, u32[]{:S(2)}, u32[]{:S(2)}) collective-permute-start(bf16[4,2,16,896]{3,2,1,0:T(8,128)(2,1)S(1)} %get-tuple-element.13), channel_id=1, source_target_pairs={{0,1},{1,0},{2,3},{3,2},{4,5},{5,4},{6,7},{7,6},{8,9},{9,8},{10,11... | collective-permute-start | bytes 688136 | tf_op jit(solution)/shard_map/ppermute | solution.py:494
  3.6 1.1 %collective-permute-done.got_ref = bf16[4,2,16,896]{3,2,1,0:T(8,128)(2,1)S(1)} collective-permute-done((bf16[4,2,16,896]{3,2,1,0:T(8,128)(2,1)S(1)}, bf16[4,2,16,896]{3,2,1,0:T(8,128)(2,1)S(1)}, u32[]{:S(2)}, u32[]{:S(2)}) %collective-permute-start) | collective-permute-done | bytes 229408 | tf_op jit(solution)/shard_map/ppermute | solution.py:494
  4.7 0.1 pair.1
  4.8 3.0 %collective-permute-start.2 = (bf16[2,16,1408]{2,1,0:T(8,128)(2,1)S(1)}, bf16[2,16,1408]{2,1,0:T(8,128)(2,1)S(1)}, u32[]{:S(2)}, u32[]{:S(2)}) collective-permute-start(bf16[2,16,1408]{2,1,0:T(8,128)(2,1)S(1)} %get-tuple-element.16), channel_id=1, source_target_pairs={{0,4},{1,7},{2,6},{3,5},{4,0},{5,3},{6,2},{7,1},{8,12},{9,15},{10,... | collective-permute-start | bytes 270344 | tf_op jit(solution)/shard_map/ppermute | solution.py:508
  7.8 2.6 %collective-permute-start.3 = (bf16[2,16,1408]{2,1,0:T(8,128)(2,1)S(1)}, bf16[2,16,1408]{2,1,0:T(8,128)(2,1)S(1)}, u32[]{:S(2)}, u32[]{:S(2)}) collective-permute-start(bf16[2,16,1408]{2,1,0:T(8,128)(2,1)S(1)} %get-tuple-element.17), channel_id=1, source_target_pairs={{0,8},{1,11},{2,10},{3,9},{4,12},{5,15},{6,14},{7,13},{8,0},{9,3},... | collective-permute-start | bytes 270344 | tf_op jit(solution)/shard_map/ppermute | solution.py:508
  10.4 0.0 collective-permute-start.4
  10.4 0.0 copy-start
  10.4 0.0 copy-start.1
  10.4 0.0 copy-start.2
  10.4 0.0 copy-start.3
  10.4 1.8 %collective-permute-start.1 = (bf16[16,1408]{1,0:T(8,128)(2,1)S(1)}, bf16[16,1408]{1,0:T(8,128)(2,1)S(1)}, u32[]{:S(2)}, u32[]{:S(2)}) collective-permute-start(bf16[16,1408]{1,0:T(8,128)(2,1)S(1)} %get-tuple-element.15), channel_id=1, source_target_pairs={{0,2},{1,3},{2,0},{3,1},{4,6},{5,7},{6,4},{7,5},{8,10},{9,11},{10,... | collective-permute-start | bytes 135176 | tf_op jit(solution)/shard_map/ppermute | solution.py:508
  12.2 2.8 %collective-permute-done.1.refs_0_.near_ref = bf16[16,1408]{1,0:T(8,128)(2,1)S(1)} collective-permute-done((bf16[16,1408]{1,0:T(8,128)(2,1)S(1)}, bf16[16,1408]{1,0:T(8,128)(2,1)S(1)}, u32[]{:S(2)}, u32[]{:S(2)}) %collective-permute-start.1) | collective-permute-done | bytes 45088 | tf_op jit(solution)/shard_map/ppermute | solution.py:508
  14.9 0.0 collective-permute-done.2.refs_1_.refs_0_
  14.9 3.0 %collective-permute-done.3.refs_2_.refs_1_ = bf16[2,16,1408]{2,1,0:T(8,128)(2,1)S(1)} collective-permute-done((bf16[2,16,1408]{2,1,0:T(8,128)(2,1)S(1)}, bf16[2,16,1408]{2,1,0:T(8,128)(2,1)S(1)}, u32[]{:S(2)}, u32[]{:S(2)}) %collective-permute-start.3) | collective-permute-done | bytes 90144 | tf_op jit(solution)/shard_map/ppermute | solution.py:508
  18.0 0.0 collective-permute-done.4.refs_3_.refs_2_
  18.0 0.6 %collective-permute-start.5 = (bf16[3,16,1408]{2,1,0:T(8,128)(2,1)S(1)}, bf16[3,16,1408]{2,1,0:T(8,128)(2,1)S(1)}, u32[]{:S(2)}, u32[]{:S(2)}) collective-permute-start(bf16[3,16,1408]{2,1,0:T(8,128)(2,1)S(1)} %relay.1), channel_id=1, source_target_pairs={{0,1},{1,0},{2,3},{3,2},{4,5},{5,4},{6,7},{7,6},{8,9},{9,8},{10,11... | collective-permute-start | bytes 405512 | tf_op jit(solution)/shard_map/ppermute | solution.py:517
  18.6 1.0 %collective-permute-done.5.refs_3_ = bf16[3,16,1408]{2,1,0:T(8,128)(2,1)S(1)} collective-permute-done((bf16[3,16,1408]{2,1,0:T(8,128)(2,1)S(1)}, bf16[3,16,1408]{2,1,0:T(8,128)(2,1)S(1)}, u32[]{:S(2)}, u32[]{:S(2)}) %collective-permute-start.5) | collective-permute-done | bytes 135200 | tf_op jit(solution)/shard_map/ppermute | solution.py:517
  19.5 0.0 copy-done
  19.5 0.0 copy-done.1
  19.5 0.0 copy-done.2
  19.6 0.0 copy-done.3
  19.6 2.6 %spectrum.1 = f32[16,4096]{1,0:T(8,128)} custom-call(bf16[16,1408]{1,0:T(8,128)(2,1)S(1)} %get-tuple-element.14.own_ref, bf16[16,1408]{1,0:T(8,128)(2,1)S(1)} %collective-permute-done.1.refs_0_.near_ref, bf16[2,16,1408]{2,1,0:T(8,128)(2,1)S(1)} %collective-permute-done.2.refs_1_.refs_0_, bf16[2,16,1408]{2,1,0:T(8,128)(2,1)S(1)} %collective-permute-done.3.refs_2_.refs_1_, ...), custom_call_target="tpu_custom_call" | custom-call | tf_op jit(solution)/shard_map/spectrum/pallas_call | solution.py:523
  (1 shorter events, 0.0 us)
Async XLA Ops:
  3.0 1.7 %collective-permute-start = (bf16[4,2,16,896]{3,2,1,0:T(8,128)(2,1)S(1)}, bf16[4,2,16,896]{3,2,1,0:T(8,128)(2,1)S(1)}, u32[]{:S(2)}, u32[]{:S(2)}) collective-permute-start(bf16[4,2,16,896]{3,2,1,0:T(8,128)(2,1)S(1)} %get-tuple-element.13), channel_id=1, source_target_pairs={{0,1},{1,0},{2,3},{3,2},{4,5},{5,4},{6,7},{7,6},{8,9},{9,8},{10,11... | collective-permute-start | bytes 688136 | tf_op jit(solution)/shard_map/ppermute | solution.py:494
  4.8 10.1 %collective-permute-start.2 = (bf16[2,16,1408]{2,1,0:T(8,128)(2,1)S(1)}, bf16[2,16,1408]{2,1,0:T(8,128)(2,1)S(1)}, u32[]{:S(2)}, u32[]{:S(2)}) collective-permute-start(bf16[2,16,1408]{2,1,0:T(8,128)(2,1)S(1)} %get-tuple-element.16), channel_id=1, source_target_pairs={{0,4},{1,7},{2,6},{3,5},{4,0},{5,3},{6,2},{7,1},{8,12},{9,15},{10,... | collective-permute-start | bytes 270344 | tf_op jit(solution)/shard_map/ppermute | solution.py:508
  7.8 10.2 %collective-permute-start.3 = (bf16[2,16,1408]{2,1,0:T(8,128)(2,1)S(1)}, bf16[2,16,1408]{2,1,0:T(8,128)(2,1)S(1)}, u32[]{:S(2)}, u32[]{:S(2)}) collective-permute-start(bf16[2,16,1408]{2,1,0:T(8,128)(2,1)S(1)} %get-tuple-element.17), channel_id=1, source_target_pairs={{0,8},{1,11},{2,10},{3,9},{4,12},{5,15},{6,14},{7,13},{8,0},{9,3},... | collective-permute-start | bytes 270344 | tf_op jit(solution)/shard_map/ppermute | solution.py:508
  10.4 7.6 %collective-permute-start.4 = (bf16[2,16,1408]{2,1,0:T(8,128)(2,1)S(1)}, bf16[2,16,1408]{2,1,0:T(8,128)(2,1)S(1)}, u32[]{:S(2)}, u32[]{:S(2)}) collective-permute-start(bf16[2,16,1408]{2,1,0:T(8,128)(2,1)S(1)} %get-tuple-element.18), channel_id=1, source_target_pairs={{0,12},{1,15},{2,14},{3,13},{4,8},{5,11},{6,10},{7,9},{8,4},{9,7},... | collective-permute-start | bytes 270344 | tf_op jit(solution)/shard_map/ppermute | solution.py:508
  10.4 9.1 %copy-start = (bf16[128,128]{1,0:T(8,128)(2,1)S(1)}, bf16[128,128]{1,0:T(8,128)(2,1)}, u32[]{:S(2)}) copy-start(bf16[128,128]{1,0:T(8,128)(2,1)} %constant.11.clone.refs_7_) | copy-start | bytes 98308
  10.4 9.1 %copy-start.1 = (f32[64,128]{1,0:T(8,128)S(1)}, f32[64,128]{1,0:T(8,128)}, u32[]{:S(2)}) copy-start(f32[64,128]{1,0:T(8,128)} %constant.10.clone.refs_6_) | copy-start | bytes 98308
  10.4 9.1 %copy-start.2 = (f32[64,128]{1,0:T(8,128)S(1)}, f32[64,128]{1,0:T(8,128)}, u32[]{:S(2)}) copy-start(f32[64,128]{1,0:T(8,128)} %constant.9.clone.refs_5_) | copy-start | bytes 98308
  10.4 9.1 %copy-start.3 = (bf16[128,88]{1,0:T(8,128)(2,1)S(1)}, bf16[128,88]{1,0:T(8,128)(2,1)}, u32[]{:S(2)}) copy-start(bf16[128,88]{1,0:T(8,128)(2,1)} %constant.8.clone.refs_4_) | copy-start | bytes 67588
  10.4 4.5 %collective-permute-start.1 = (bf16[16,1408]{1,0:T(8,128)(2,1)S(1)}, bf16[16,1408]{1,0:T(8,128)(2,1)S(1)}, u32[]{:S(2)}, u32[]{:S(2)}) collective-permute-start(bf16[16,1408]{1,0:T(8,128)(2,1)S(1)} %get-tuple-element.15), channel_id=1, source_target_pairs={{0,2},{1,3},{2,0},{3,1},{4,6},{5,7},{6,4},{7,5},{8,10},{9,11},{10,... | collective-permute-start | bytes 135176 | tf_op jit(solution)/shard_map/ppermute | solution.py:508
  18.0 1.5 %collective-permute-start.5 = (bf16[3,16,1408]{2,1,0:T(8,128)(2,1)S(1)}, bf16[3,16,1408]{2,1,0:T(8,128)(2,1)S(1)}, u32[]{:S(2)}, u32[]{:S(2)}) collective-permute-start(bf16[3,16,1408]{2,1,0:T(8,128)(2,1)S(1)} %relay.1), channel_id=1, source_target_pairs={{0,1},{1,0},{2,3},{3,2},{4,5},{5,4},{6,7},{7,6},{8,9},{9,8},{10,11... | collective-permute-start | bytes 405512 | tf_op jit(solution)/shard_map/ppermute | solution.py:517

commit v2 on v1

--- a/solution.py
+++ b/solution.py
@@ -380,41 +380,73 @@
             slot_ref[pl.ds(slot + tile, rows, stride=pitch), :] = ref[
                 at + (slice(None), slice(tile * LANES, (tile + 1) * LANES))
             ].astype(jnp.float32)
-    lane = lax.broadcasted_iota(jnp.int32, (halves // 2, LANES), 1)
-    sign = jnp.where(lax.broadcasted_iota(jnp.int32, (halves, LANES), 1) < bins, 1.0, -1.0)
+    lines = halves // 2
+    lane = lax.broadcasted_iota(jnp.int32, (lines, LANES), 1)
+    group = 4
     stores = []
-    for row in range(rows):
-        series = slot_ref[row * pitch : row * pitch + used, :].astype(jnp.bfloat16)
-        turned = jnp.dot(first_ref[...], series, preferred_element_type=jnp.float32)
-        real, imag = turned[:bins], turned[bins:]
-        twisted_re = (real * cos_ref[...] - imag * sin_ref[...]).astype(jnp.bfloat16)
-        twisted_im = (-imag * cos_ref[...] - real * sin_ref[...]).astype(jnp.bfloat16)
-        twisted = jnp.concatenate([twisted_re, twisted_im], axis=0)
+
+    def first_stage(start):
+        series = jnp.concatenate(
+            [
+                slot_ref[row * pitch : row * pitch + used, :].astype(jnp.bfloat16)
+                for row in range(start, start + group)
+            ],
+            axis=1,
+        )
+        return jnp.dot(first_ref[...], series, preferred_element_type=jnp.float32)
+
+    def twist(turned):
+        twisted = []
+        for at in range(group):
+            real = turned[:bins, at * LANES : (at + 1) * LANES]
+            imag = turned[bins:, at * LANES : (at + 1) * LANES]
+            twisted.append(
+                jnp.concatenate(
+                    [
+                        (real * cos_ref[...] - imag * sin_ref[...]).astype(jnp.bfloat16),
+                        (-imag * cos_ref[...] - real * sin_ref[...]).astype(jnp.bfloat16),
+                    ],
+                    axis=1,
+                )
+            )
+        return jnp.concatenate(twisted, axis=0)
+
+    def last_stage(start, twisted):
         mixed = lax.dot_general(
             third_ref[...], twisted, (((1,), (1,)), ((), ())), preferred_element_type=jnp.float32
         )
-        value = mixed[:halves] + sign * pltpu.roll(mixed[halves:], bins, axis=1)
-        square = value * value
-        power = (square + pltpu.roll(square, bins, axis=1)) * scale
-        line = jnp.where(lane < bins, power[: halves // 2], power[halves // 2 :])
-        flat_ref[
-            pl.ds(row // 8 * 8 * (halves // 2) + row % 8, halves // 2, stride=8), :
-        ] = line
+        real, imag = mixed[:halves], mixed[halves:]
+        power = (real * real + imag * imag) * scale
+        for at in range(0, group, 2):
+            both = power[:, at * bins : at * bins + LANES]
+            even, odd = both[:lines], both[lines:]
+            left = jnp.where(lane < bins, even, pltpu.roll(odd, bins, axis=1))
+            right = jnp.where(lane < bins, pltpu.roll(even, bins, axis=1), odd)
+            for row, line in ((start + at, left), (start + at + 1, right)):
+                flat_ref[pl.ds(row // 8 * 8 * lines + row % 8, lines, stride=8), :] = line
+        row = start + group - 1
         if row % 8 == 7:
-            group = row // 8
-            for tile in range(halves // 2):
-                at = (group * (halves // 2) + tile) * 8
-                lines_ref[group * 8 : group * 8 + 8, tile * LANES : (tile + 1) * LANES] = flat_ref[
+            part = row // 8
+            for tile in range(lines):
+                at = (part * lines + tile) * 8
+                lines_ref[part * 8 : part * 8 + 8, tile * LANES : (tile + 1) * LANES] = flat_ref[
                     at : at + 8, :
                 ]
             stores.append(
                 pltpu.make_async_copy(
-                    lines_ref.at[pl.ds(group * 8, 8)],
-                    out_ref.at[pl.ds(group * 8, 8)],
-                    sems.at[group],
+                    lines_ref.at[pl.ds(part * 8, 8)],
+                    out_ref.at[pl.ds(part * 8, 8)],
+                    sems.at[part],
                 )
             )
             stores[-1].start()
+
+    turned = first_stage(0)
+    for start in range(0, rows, group):
+        twisted = twist(turned)
+        if start + group < rows:
+            turned = first_stage(start + group)
+        last_stage(start, twisted)
     for store in stores:
         store.wait()
 
@@ -439,7 +471,8 @@
     two = angle(k[:, None] * n[None, :], SAMPLES)
     m = np.concatenate([m[0::2], m[1::2]])
     three = angle(m[:, None] * n[None, :], LANES)
-    third = np.concatenate([np.cos(three), np.sin(three)], axis=0)
+    cos_three, sin_three = np.cos(three), np.sin(three)
+    third = np.block([[cos_three, sin_three], [-sin_three, cos_three]])
     return (
         jnp.asarray(first, jnp.bfloat16),
         jnp.asarray(np.cos(two), jnp.float32),

time: 22.3 us -> 21.1 us (0.946)
  Pallas kernels: 5.72 us -> 4.52 us
    pallas_call x1, Pallas kernels: 2.59 us -> 1.39 us  [slice_plan(): pl.pallas_call(functools.partial(spectrum_kernel, rings, 1.0 / (SAMPLES *...]
where the time goes in v2:
time: 21.1 us; the launch traced here: 20.9 us
  starting transfers between devices  8.46 us (40%)
  waiting for transfers between devices  7.9 us (37%)
  Pallas kernels  4.52 us (21%)
    ppermute x4, starting transfers between devices, slice_plan(): arrived.append(on_chip(lax.ppermute(message, 'sub', route)))  7.35 us
    ppermute x4, waiting for transfers between devices, slice_plan(): arrived.append(on_chip(lax.ppermute(message, 'sub', route)))  5.8 us
    pallas_call x1, Pallas kernels, slice_plan(): pl.pallas_call(functools.partial(tree_kernel, owners, margin), out_shape=...  3.03 us
    pallas_call x1, Pallas kernels, slice_plan(): pl.pallas_call(functools.partial(spectrum_kernel, rings, 1.0 / (SAMPLES *...  1.39 us
    ppermute x1, waiting for transfers between devices, slice_plan(): got = on_chip(lax.ppermute(send, 'sub', beside))  1.12 us
    ppermute x1, waiting for transfers between devices, slice_plan(): relay = on_chip(lax.ppermute(relay, 'sub', beside))  0.99 us
    ppermute x1, starting transfers between devices, slice_plan(): got = on_chip(lax.ppermute(send, 'sub', beside))  0.56 us
    ppermute x1, starting transfers between devices, slice_plan(): relay = on_chip(lax.ppermute(relay, 'sub', beside))  0.55 us
  transfers between devices with their start and end apart: 6, of which 4 were waited for; matrix products, arithmetic and copies ran while one was open for 0% of the time, Pallas kernels for 0%

profile of v2, /device:TPU:0, one launch (start us, length us, event | category | flops | bytes accessed | tf_op | source)
XLA Modules:
  0.0 20.9 jit_solution(6784964379815774080)
XLA Ops:
  0.0 3.0 %tree.1 = (bf16[4,2,16,896]{3,2,1,0:T(8,128)(2,1)S(1)}, bf16[4,2,16,896]{3,2,1,0:T(8,128)(2,1)S(1)}) custom-call(bf16[528,512]{1,0:T(8,128)(2,1)} %samples_at.1, s32[1,512]{1,0:T(1,128)} %bitcast.1, s32[9,3,256]{2,1,0:T(4,128)} %table_at.1), custom_call_target="tpu_custom_call" | custom-call | tf_op jit(solution)/shard_map/tree/pallas_call | solution.py:507
  3.0 0.6 %collective-permute-start = (bf16[4,2,16,896]{3,2,1,0:T(8,128)(2,1)S(1)}, bf16[4,2,16,896]{3,2,1,0:T(8,128)(2,1)S(1)}, u32[]{:S(2)}, u32[]{:S(2)}) collective-permute-start(bf16[4,2,16,896]{3,2,1,0:T(8,128)(2,1)S(1)} %get-tuple-element.13), channel_id=1, source_target_pairs={{0,1},{1,0},{2,3},{3,2},{4,5},{5,4},{6,7},{7,6},{8,9},{9,8},{10,11... | collective-permute-start | bytes 688136 | tf_op jit(solution)/shard_map/ppermute | solution.py:527
  3.6 1.1 %collective-permute-done.got_ref = bf16[4,2,16,896]{3,2,1,0:T(8,128)(2,1)S(1)} collective-permute-done((bf16[4,2,16,896]{3,2,1,0:T(8,128)(2,1)S(1)}, bf16[4,2,16,896]{3,2,1,0:T(8,128)(2,1)S(1)}, u32[]{:S(2)}, u32[]{:S(2)}) %collective-permute-start) | collective-permute-done | bytes 229408 | tf_op jit(solution)/shard_map/ppermute | solution.py:527
  4.7 0.1 pair.1
  4.8 3.0 %collective-permute-start.2 = (bf16[2,16,1408]{2,1,0:T(8,128)(2,1)S(1)}, bf16[2,16,1408]{2,1,0:T(8,128)(2,1)S(1)}, u32[]{:S(2)}, u32[]{:S(2)}) collective-permute-start(bf16[2,16,1408]{2,1,0:T(8,128)(2,1)S(1)} %get-tuple-element.16), channel_id=1, source_target_pairs={{0,4},{1,7},{2,6},{3,5},{4,0},{5,3},{6,2},{7,1},{8,12},{9,15},{10,... | collective-permute-start | bytes 270344 | tf_op jit(solution)/shard_map/ppermute | solution.py:541
  7.8 2.6 %collective-permute-start.3 = (bf16[2,16,1408]{2,1,0:T(8,128)(2,1)S(1)}, bf16[2,16,1408]{2,1,0:T(8,128)(2,1)S(1)}, u32[]{:S(2)}, u32[]{:S(2)}) collective-permute-start(bf16[2,16,1408]{2,1,0:T(8,128)(2,1)S(1)} %get-tuple-element.17), channel_id=1, source_target_pairs={{0,8},{1,11},{2,10},{3,9},{4,12},{5,15},{6,14},{7,13},{8,0},{9,3},... | collective-permute-start | bytes 270344 | tf_op jit(solution)/shard_map/ppermute | solution.py:541
  10.4 0.0 collective-permute-start.4
  10.4 0.0 copy-start
  10.4 0.0 copy-start.1
  10.4 0.0 copy-start.2
  10.4 0.0 copy-start.3
  10.4 1.8 %collective-permute-start.1 = (bf16[16,1408]{1,0:T(8,128)(2,1)S(1)}, bf16[16,1408]{1,0:T(8,128)(2,1)S(1)}, u32[]{:S(2)}, u32[]{:S(2)}) collective-permute-start(bf16[16,1408]{1,0:T(8,128)(2,1)S(1)} %get-tuple-element.15), channel_id=1, source_target_pairs={{0,2},{1,3},{2,0},{3,1},{4,6},{5,7},{6,4},{7,5},{8,10},{9,11},{10,... | collective-permute-start | bytes 135176 | tf_op jit(solution)/shard_map/ppermute | solution.py:541
  12.2 2.8 %collective-permute-done.1.refs_0_.near_ref = bf16[16,1408]{1,0:T(8,128)(2,1)S(1)} collective-permute-done((bf16[16,1408]{1,0:T(8,128)(2,1)S(1)}, bf16[16,1408]{1,0:T(8,128)(2,1)S(1)}, u32[]{:S(2)}, u32[]{:S(2)}) %collective-permute-start.1) | collective-permute-done | bytes 45088 | tf_op jit(solution)/shard_map/ppermute | solution.py:541
  14.9 0.0 collective-permute-done.2.refs_1_.refs_0_
  14.9 3.0 %collective-permute-done.3.refs_2_.refs_1_ = bf16[2,16,1408]{2,1,0:T(8,128)(2,1)S(1)} collective-permute-done((bf16[2,16,1408]{2,1,0:T(8,128)(2,1)S(1)}, bf16[2,16,1408]{2,1,0:T(8,128)(2,1)S(1)}, u32[]{:S(2)}, u32[]{:S(2)}) %collective-permute-start.3) | collective-permute-done | bytes 90144 | tf_op jit(solution)/shard_map/ppermute | solution.py:541
  18.0 0.0 collective-permute-done.4.refs_3_.refs_2_
  18.0 0.6 %collective-permute-start.5 = (bf16[3,16,1408]{2,1,0:T(8,128)(2,1)S(1)}, bf16[3,16,1408]{2,1,0:T(8,128)(2,1)S(1)}, u32[]{:S(2)}, u32[]{:S(2)}) collective-permute-start(bf16[3,16,1408]{2,1,0:T(8,128)(2,1)S(1)} %relay.1), channel_id=1, source_target_pairs={{0,1},{1,0},{2,3},{3,2},{4,5},{5,4},{6,7},{7,6},{8,9},{9,8},{10,11... | collective-permute-start | bytes 405512 | tf_op jit(solution)/shard_map/ppermute | solution.py:550
  18.6 1.0 %collective-permute-done.5.refs_3_ = bf16[3,16,1408]{2,1,0:T(8,128)(2,1)S(1)} collective-permute-done((bf16[3,16,1408]{2,1,0:T(8,128)(2,1)S(1)}, bf16[3,16,1408]{2,1,0:T(8,128)(2,1)S(1)}, u32[]{:S(2)}, u32[]{:S(2)}) %collective-permute-start.5) | collective-permute-done | bytes 135200 | tf_op jit(solution)/shard_map/ppermute | solution.py:550
  19.5 0.0 copy-done
  19.5 0.0 copy-done.1
  19.5 0.0 copy-done.2
  19.6 0.0 copy-done.3
  19.6 1.4 %spectrum.1 = f32[16,4096]{1,0:T(8,128)} custom-call(bf16[16,1408]{1,0:T(8,128)(2,1)S(1)} %get-tuple-element.14.own_ref, bf16[16,1408]{1,0:T(8,128)(2,1)S(1)} %collective-permute-done.1.refs_0_.near_ref, bf16[2,16,1408]{2,1,0:T(8,128)(2,1)S(1)} %collective-permute-done.2.refs_1_.refs_0_, bf16[2,16,1408]{2,1,0:T(8,128)(2,1)S(1)} %collective-permute-done.3.refs_2_.refs_1_, ...), custom_call_target="tpu_custom_call" | custom-call | tf_op jit(solution)/shard_map/spectrum/pallas_call | solution.py:556
  (1 shorter events, 0.0 us)
Async XLA Ops:
  3.0 1.7 %collective-permute-start = (bf16[4,2,16,896]{3,2,1,0:T(8,128)(2,1)S(1)}, bf16[4,2,16,896]{3,2,1,0:T(8,128)(2,1)S(1)}, u32[]{:S(2)}, u32[]{:S(2)}) collective-permute-start(bf16[4,2,16,896]{3,2,1,0:T(8,128)(2,1)S(1)} %get-tuple-element.13), channel_id=1, source_target_pairs={{0,1},{1,0},{2,3},{3,2},{4,5},{5,4},{6,7},{7,6},{8,9},{9,8},{10,11... | collective-permute-start | bytes 688136 | tf_op jit(solution)/shard_map/ppermute | solution.py:527
  4.8 10.1 %collective-permute-start.2 = (bf16[2,16,1408]{2,1,0:T(8,128)(2,1)S(1)}, bf16[2,16,1408]{2,1,0:T(8,128)(2,1)S(1)}, u32[]{:S(2)}, u32[]{:S(2)}) collective-permute-start(bf16[2,16,1408]{2,1,0:T(8,128)(2,1)S(1)} %get-tuple-element.16), channel_id=1, source_target_pairs={{0,4},{1,7},{2,6},{3,5},{4,0},{5,3},{6,2},{7,1},{8,12},{9,15},{10,... | collective-permute-start | bytes 270344 | tf_op jit(solution)/shard_map/ppermute | solution.py:541
  7.8 10.2 %collective-permute-start.3 = (bf16[2,16,1408]{2,1,0:T(8,128)(2,1)S(1)}, bf16[2,16,1408]{2,1,0:T(8,128)(2,1)S(1)}, u32[]{:S(2)}, u32[]{:S(2)}) collective-permute-start(bf16[2,16,1408]{2,1,0:T(8,128)(2,1)S(1)} %get-tuple-element.17), channel_id=1, source_target_pairs={{0,8},{1,11},{2,10},{3,9},{4,12},{5,15},{6,14},{7,13},{8,0},{9,3},... | collective-permute-start | bytes 270344 | tf_op jit(solution)/shard_map/ppermute | solution.py:541
  10.4 7.6 %collective-permute-start.4 = (bf16[2,16,1408]{2,1,0:T(8,128)(2,1)S(1)}, bf16[2,16,1408]{2,1,0:T(8,128)(2,1)S(1)}, u32[]{:S(2)}, u32[]{:S(2)}) collective-permute-start(bf16[2,16,1408]{2,1,0:T(8,128)(2,1)S(1)} %get-tuple-element.18), channel_id=1, source_target_pairs={{0,12},{1,15},{2,14},{3,13},{4,8},{5,11},{6,10},{7,9},{8,4},{9,7},... | collective-permute-start | bytes 270344 | tf_op jit(solution)/shard_map/ppermute | solution.py:541
  10.4 9.1 %copy-start = (bf16[128,256]{1,0:T(8,128)(2,1)S(1)}, bf16[128,256]{1,0:T(8,128)(2,1)}, u32[]{:S(2)}) copy-start(bf16[128,256]{1,0:T(8,128)(2,1)} %constant.11.clone.refs_7_) | copy-start | bytes 196612
  10.4 9.1 %copy-start.1 = (f32[64,128]{1,0:T(8,128)S(1)}, f32[64,128]{1,0:T(8,128)}, u32[]{:S(2)}) copy-start(f32[64,128]{1,0:T(8,128)} %constant.10.clone.refs_6_) | copy-start | bytes 98308
  10.4 9.1 %copy-start.2 = (f32[64,128]{1,0:T(8,128)S(1)}, f32[64,128]{1,0:T(8,128)}, u32[]{:S(2)}) copy-start(f32[64,128]{1,0:T(8,128)} %constant.9.clone.refs_5_) | copy-start | bytes 98308
  10.4 9.1 %copy-start.3 = (bf16[128,88]{1,0:T(8,128)(2,1)S(1)}, bf16[128,88]{1,0:T(8,128)(2,1)}, u32[]{:S(2)}) copy-start(bf16[128,88]{1,0:T(8,128)(2,1)} %constant.8.clone.refs_4_) | copy-start | bytes 67588
  10.4 4.5 %collective-permute-start.1 = (bf16[16,1408]{1,0:T(8,128)(2,1)S(1)}, bf16[16,1408]{1,0:T(8,128)(2,1)S(1)}, u32[]{:S(2)}, u32[]{:S(2)}) collective-permute-start(bf16[16,1408]{1,0:T(8,128)(2,1)S(1)} %get-tuple-element.15), channel_id=1, source_target_pairs={{0,2},{1,3},{2,0},{3,1},{4,6},{5,7},{6,4},{7,5},{8,10},{9,11},{10,... | collective-permute-start | bytes 135176 | tf_op jit(solution)/shard_map/ppermute | solution.py:541
  18.0 1.5 %collective-permute-start.5 = (bf16[3,16,1408]{2,1,0:T(8,128)(2,1)S(1)}, bf16[3,16,1408]{2,1,0:T(8,128)(2,1)S(1)}, u32[]{:S(2)}, u32[]{:S(2)}) collective-permute-start(bf16[3,16,1408]{2,1,0:T(8,128)(2,1)S(1)} %relay.1), channel_id=1, source_target_pairs={{0,1},{1,0},{2,3},{3,2},{4,5},{5,4},{6,7},{7,6},{8,9},{9,8},{10,11... | collective-permute-start | bytes 405512 | tf_op jit(solution)/shard_map/ppermute | solution.py:550

commit v3 on v2

--- a/solution.py
+++ b/solution.py
@@ -158,8 +158,8 @@
 
 
 def tree_kernel(
-    owners, margin, samples_at, order_at, table_at, keep_ref, send_ref, raw_ref, order_ref,
-    table_ref, first_ref, pick_ref, cur_ref, picked_ref, final_ref, turned_ref, sems,
+    owners, margin, samples_at, order_at, table_at, turned_ref, send_ref, raw_ref, order_ref,
+    table_ref, first_ref, pick_ref, cur_ref, picked_ref, final_ref, sems,
 ):
     window, channels = raw_ref.shape
     levels, _, dmax = table_ref.shape
@@ -318,29 +318,34 @@
         for time in range(final_ref.shape[0] // LANES):
             lanes = slice(time * LANES, (time + 1) * LANES)
             turned_ref[at, lanes] = final_ref[lanes, at].T
-    me = lax.axis_index("sub")
-    bits = (owners - 1).bit_length()
+    other = 1 - (lax.axis_index("sub") & 1)
+    for ring in range(send_ref.shape[0]):
+        for relay in range(2):
+            send_ref[ring, relay] = turned_ref[rows_for(owners, dmax, ring, relay, other), :]
+
+
+def rows_for(owners, dmax, ring, relay, core):
+    chip, side = (2 * ring + core, core ^ relay) if ring else (relay, core)
+    owner = ((lax.axis_index("sub") >> 1) ^ chip) << 1 | side
     rows = dmax // owners
-    for ref, core in ((keep_ref, me & 1), (send_ref, 1 - (me & 1))):
-        for ring in range(ref.shape[0]):
-            for relay in range(2):
-                chip, side = (2 * ring + core, core ^ relay) if ring else (relay, core)
-                block = reverse_bits(((me >> 1) ^ chip) << 1 | side, bits)
-                ref[ring, relay] = turned_ref[pl.ds(pl.multiple_of(block * rows, rows), rows), :]
-
-
-def pair_kernel(apart, keep_ref, got_ref, own_ref, near_ref, *message_refs):
-    lower = lax.axis_index("sub") & 1 == 0
-    tiles = keep_ref.shape[-1] // LANES
-    for ring in range(keep_ref.shape[0]):
+    block = reverse_bits(owner, (owners - 1).bit_length())
+    return pl.ds(pl.multiple_of(block * rows, rows), rows)
+
+
+def pair_kernel(owners, apart, turned_ref, got_ref, own_ref, near_ref, *message_refs):
+    core = lax.axis_index("sub") & 1
+    lower = core == 0
+    tiles = turned_ref.shape[-1] // LANES
+    for ring in range(got_ref.shape[0]):
         for relay in range(2):
+            rows = rows_for(owners, turned_ref.shape[0], ring, relay, core)
             for tile in range(apart + tiles):
                 total = None
                 for start, mine in ((0, lower), (apart, ~lower)):
                     if start <= tile < start + tiles:
                         lanes = slice((tile - start) * LANES, (tile - start + 1) * LANES)
                         part = jnp.where(
-                            mine, keep_ref[ring, relay, :, lanes], got_ref[ring, relay, :, lanes]
+                            mine, turned_ref[rows, lanes], got_ref[ring, relay, :, lanes]
                         ).astype(jnp.float32)
                         total = part if total is None else total + part
                 total = total.astype(own_ref.dtype)
@@ -351,17 +356,13 @@
                     (near_ref if relay else own_ref)[:, lanes] = total
 
 
-def relay_kernel(*refs):
-    for at, ref in enumerate(refs[1:-1]):
-        refs[-1][at] = ref[1]
-
-
 def spectrum_kernel(
     rings, scale, own_ref, near_ref, *refs
 ):
     message_refs, refs = refs[: rings - 1], refs[rings - 1 :]
-    relay_ref, first_ref, cos_ref, sin_ref, third_ref, out_ref = refs[:6]
-    slot_ref, flat_ref, lines_ref, sems = refs[6:]
+    relay_refs, refs = refs[: rings - 1], refs[rings - 1 :]
+    first_ref, cos_ref, sin_ref, third_ref, out_ref = refs[:5]
+    slot_ref, flat_ref, lines_ref, sems = refs[5:]
     rows, width = own_ref.shape
     tiles = width // LANES
     pitch = slot_ref.shape[0] // rows
@@ -373,7 +374,7 @@
     sources = [(own_ref, (), 0), (near_ref, (), 1)]
     for ring in range(1, rings):
         sources.append((message_refs[ring - 1], (0,), 2 * ring + core))
-        sources.append((relay_ref, (ring - 1,), 2 * ring + 1 - core))
+        sources.append((relay_refs[ring - 1], (1,), 2 * ring + 1 - core))
     for ref, at, apart in sources:
         slot = ((me >> 1) ^ apart) * tiles
         for tile in range(tiles):
@@ -504,9 +505,9 @@
     wide = width + apart * LANES
     vmem = pl.BlockSpec(memory_space=pltpu.VMEM)
     half = pltpu.VMEM((rings, 2, rows, width), jnp.bfloat16)
-    keep, send = pl.pallas_call(
+    turned, send = pl.pallas_call(
         functools.partial(tree_kernel, owners, margin),
-        out_shape=[half, half],
+        out_shape=[pltpu.VMEM((dmax, width), jnp.bfloat16), half],
         in_specs=[pl.BlockSpec(memory_space=pl.ANY)] * 3,
         out_specs=[vmem, vmem],
         scratch_shapes=[
@@ -518,7 +519,6 @@
             pltpu.VMEM((kept, dmax), jnp.bfloat16),
             pltpu.VMEM((kept, 2 * dmax), jnp.float32),
             pltpu.VMEM((width, dmax), jnp.bfloat16),
-            pltpu.VMEM((dmax, width), jnp.bfloat16),
             pltpu.SemaphoreType.DMA((3,)),
         ],
         name="tree",
@@ -528,26 +528,21 @@
     block = pltpu.VMEM((rows, wide), jnp.bfloat16)
     message = pltpu.VMEM((2, rows, wide), jnp.bfloat16)
     own, near, *messages = pl.pallas_call(
-        functools.partial(pair_kernel, apart),
+        functools.partial(pair_kernel, owners, apart),
         out_shape=[block, block] + [message] * (rings - 1),
         in_specs=[vmem] * 2,
         out_specs=[vmem] * (rings + 1),
         name="pair",
-    )(on_chip(keep), got)
+    )(on_chip(turned), got)
     arrived = []
     for ring in range(rings):
         route = [(a, a ^ (2 * (2 * ring + a % 2) if ring else 2)) for a in range(owners)]
         message = messages[ring - 1] if ring else near
         arrived.append(on_chip(lax.ppermute(message, "sub", route)))
     near, *arrived = arrived
-    relay = pl.pallas_call(
-        relay_kernel,
-        out_shape=pltpu.VMEM((rings - 1, rows, wide), jnp.bfloat16),
-        in_specs=[vmem] * rings,
-        out_specs=vmem,
-        name="relay",
-    )(near, *arrived)
-    relay = on_chip(lax.ppermute(relay, "sub", beside))
+    relayed = []
+    for ring in range(1, rings):
+        relayed.append(on_chip(lax.ppermute(arrived[ring - 1], "sub", beside)))
     pairs = owners // 2
     tables = [
         on_chip(table) for table in spectrum_tables(pairs, 2 * window, margin, wide // LANES)
@@ -556,7 +551,7 @@
     return pl.pallas_call(
         functools.partial(spectrum_kernel, rings, 1.0 / (SAMPLES * channels)),
         out_shape=jax.ShapeDtypeStruct((rows, SAMPLES // 2), jnp.float32),
-        in_specs=[vmem] * (rings + 6),
+        in_specs=[vmem] * (2 * rings + 4),
         out_specs=pl.BlockSpec(memory_space=pl.ANY),
         scratch_shapes=[
             pltpu.VMEM((rows * pitch, LANES), jnp.float32),
@@ -565,7 +560,7 @@
             pltpu.SemaphoreType.DMA((rows // 8,)),
         ],
         name="spectrum",
-    )(on_chip(own), near, *arrived, relay, *tables)
+    )(on_chip(own), near, *arrived, *relayed, *tables)
 
 
 def local(samples, channel_order, merge_table):

time: 21.1 us -> 24.1 us (1.14)
  waiting for transfers between devices: 7.9 us -> 10.3 us
  starting transfers between devices: 8.46 us -> 9.11 us
    ppermute x4, waiting for transfers between devices: 5.8 us -> 9.18 us  [slice_plan(): arrived.append(on_chip(lax.ppermute(message, 'sub', route)))]
    ppermute x1 -> x3, waiting for transfers between devices: 0.99 us -> 0.01 us  [slice_plan(): relayed.append(on_chip(lax.ppermute(arrived[ring - 1], 'sub', beside)))]
    ppermute x1 -> x3, starting transfers between devices: 0.55 us -> 1.5 us  [slice_plan(): relayed.append(on_chip(lax.ppermute(arrived[ring - 1], 'sub', beside)))]
    ppermute x4, starting transfers between devices: 7.35 us -> 7.05 us  [slice_plan(): arrived.append(on_chip(lax.ppermute(message, 'sub', route)))]
  transfers between devices with their start and end apart: 6 -> 8, of which waited for: 4 -> 4; matrix products, arithmetic and copies ran while one was open for 0% -> 0% of each run, Pallas kernels for 0% -> 0%
where the time goes in v3:
time: 24.1 us; the launch traced here: 24 us
  waiting for transfers between devices  10.3 us (43%)
  starting transfers between devices  9.11 us (38%)
  Pallas kernels  4.5 us (19%)
    ppermute x4, waiting for transfers between devices, slice_plan(): arrived.append(on_chip(lax.ppermute(message, 'sub', route)))  9.18 us
    ppermute x4, starting transfers between devices, slice_plan(): arrived.append(on_chip(lax.ppermute(message, 'sub', route)))  7.05 us
    pallas_call x1, Pallas kernels, slice_plan(): pl.pallas_call(functools.partial(tree_kernel, owners, margin), out_shape=...  3.02 us
    ppermute x3, starting transfers between devices, slice_plan(): relayed.append(on_chip(lax.ppermute(arrived[ring - 1], 'sub', beside)))  1.5 us
    pallas_call x1, Pallas kernels, slice_plan(): pl.pallas_call(functools.partial(spectrum_kernel, rings, 1.0 / (SAMPLES *...  1.39 us
    ppermute x1, waiting for transfers between devices, slice_plan(): got = on_chip(lax.ppermute(send, 'sub', beside))  1.12 us
    ppermute x1, starting transfers between devices, slice_plan(): got = on_chip(lax.ppermute(send, 'sub', beside))  0.56 us
  transfers between devices with their start and end apart: 8, of which 4 were waited for; matrix products, arithmetic and copies ran while one was open for 0% of the time, Pallas kernels for 0%

profile of v3, /device:TPU:0, one launch (start us, length us, event | category | flops | bytes accessed | tf_op | source)
XLA Modules:
  0.0 24.0 jit_solution(13543260162950276456)
XLA Ops:
  0.0 3.0 %tree.1 = (bf16[256,896]{1,0:T(8,128)(2,1)S(1)}, bf16[4,2,16,896]{3,2,1,0:T(8,128)(2,1)S(1)}) custom-call(bf16[528,512]{1,0:T(8,128)(2,1)} %samples_at.1, s32[1,512]{1,0:T(1,128)} %bitcast.1, s32[9,3,256]{2,1,0:T(4,128)} %table_at.1), custom_call_target="tpu_custom_call" | custom-call | tf_op jit(solution)/shard_map/tree/pallas_call | solution.py:508
  3.0 0.6 %collective-permute-start = (bf16[4,2,16,896]{3,2,1,0:T(8,128)(2,1)S(1)}, bf16[4,2,16,896]{3,2,1,0:T(8,128)(2,1)S(1)}, u32[]{:S(2)}, u32[]{:S(2)}) collective-permute-start(bf16[4,2,16,896]{3,2,1,0:T(8,128)(2,1)S(1)} %get-tuple-element.13), channel_id=1, source_target_pairs={{0,1},{1,0},{2,3},{3,2},{4,5},{5,4},{6,7},{7,6},{8,9},{9,8},{10,11... | collective-permute-start | bytes 688136 | tf_op jit(solution)/shard_map/ppermute | solution.py:527
  3.6 1.1 %collective-permute-done.got_ref = bf16[4,2,16,896]{3,2,1,0:T(8,128)(2,1)S(1)} collective-permute-done((bf16[4,2,16,896]{3,2,1,0:T(8,128)(2,1)S(1)}, bf16[4,2,16,896]{3,2,1,0:T(8,128)(2,1)S(1)}, u32[]{:S(2)}, u32[]{:S(2)}) %collective-permute-start) | collective-permute-done | bytes 229408 | tf_op jit(solution)/shard_map/ppermute | solution.py:527
  4.7 0.0 copy-start
  4.7 0.0 copy-start.1
  4.7 0.0 copy-start.2
  4.7 0.0 copy-start.3
  4.7 0.1 pair.1
  4.8 3.0 %collective-permute-start.2 = (bf16[2,16,1408]{2,1,0:T(8,128)(2,1)S(1)}, bf16[2,16,1408]{2,1,0:T(8,128)(2,1)S(1)}, u32[]{:S(2)}, u32[]{:S(2)}) collective-permute-start(bf16[2,16,1408]{2,1,0:T(8,128)(2,1)S(1)} %get-tuple-element.16), channel_id=1, source_target_pairs={{0,4},{1,7},{2,6},{3,5},{4,0},{5,3},{6,2},{7,1},{8,12},{9,15},{10,... | collective-permute-start | bytes 270344 | tf_op jit(solution)/shard_map/ppermute | solution.py:541
  7.8 2.6 %collective-permute-start.3 = (bf16[2,16,1408]{2,1,0:T(8,128)(2,1)S(1)}, bf16[2,16,1408]{2,1,0:T(8,128)(2,1)S(1)}, u32[]{:S(2)}, u32[]{:S(2)}) collective-permute-start(bf16[2,16,1408]{2,1,0:T(8,128)(2,1)S(1)} %get-tuple-element.17), channel_id=1, source_target_pairs={{0,8},{1,11},{2,10},{3,9},{4,12},{5,15},{6,14},{7,13},{8,0},{9,3},... | collective-permute-start | bytes 270344 | tf_op jit(solution)/shard_map/ppermute | solution.py:541
  10.4 0.0 collective-permute-start.4
  10.4 0.3 %collective-permute-done.2.refs_0_ = bf16[2,16,1408]{2,1,0:T(8,128)(2,1)S(1)} collective-permute-done((bf16[2,16,1408]{2,1,0:T(8,128)(2,1)S(1)}, bf16[2,16,1408]{2,1,0:T(8,128)(2,1)S(1)}, u32[]{:S(2)}, u32[]{:S(2)}) %collective-permute-start.2) | collective-permute-done | bytes 90144 | tf_op jit(solution)/shard_map/ppermute | solution.py:541
  10.8 1.0 %collective-permute-start.5 = (bf16[2,16,1408]{2,1,0:T(8,128)(2,1)S(1)}, bf16[2,16,1408]{2,1,0:T(8,128)(2,1)S(1)}, u32[]{:S(2)}, u32[]{:S(2)}) collective-permute-start(bf16[2,16,1408]{2,1,0:T(8,128)(2,1)S(1)} %collective-permute-done.2.refs_0_), channel_id=1, source_target_pairs={{0,1},{1,0},{2,3},{3,2},{4,5},{5,4},{6,7},{7,6},{8,9},{9,8},{10,11... | collective-permute-start | bytes 270344 | tf_op jit(solution)/shard_map/ppermute | solution.py:545
  11.7 6.2 %collective-permute-done.3.refs_1_ = bf16[2,16,1408]{2,1,0:T(8,128)(2,1)S(1)} collective-permute-done((bf16[2,16,1408]{2,1,0:T(8,128)(2,1)S(1)}, bf16[2,16,1408]{2,1,0:T(8,128)(2,1)S(1)}, u32[]{:S(2)}, u32[]{:S(2)}) %collective-permute-start.3) | collective-permute-done | bytes 90144 | tf_op jit(solution)/shard_map/ppermute | solution.py:541
  18.0 0.5 %collective-permute-start.6 = (bf16[2,16,1408]{2,1,0:T(8,128)(2,1)S(1)}, bf16[2,16,1408]{2,1,0:T(8,128)(2,1)S(1)}, u32[]{:S(2)}, u32[]{:S(2)}) collective-permute-start(bf16[2,16,1408]{2,1,0:T(8,128)(2,1)S(1)} %collective-permute-done.3.refs_1_), channel_id=1, source_target_pairs={{0,1},{1,0},{2,3},{3,2},{4,5},{5,4},{6,7},{7,6},{8,9},{9,8},{10,11... | collective-permute-start | bytes 270344 | tf_op jit(solution)/shard_map/ppermute | solution.py:545
  18.5 0.0 collective-permute-done.4.refs_2_
  18.5 0.0 collective-permute-start.7
  18.5 1.5 %collective-permute-start.1 = (bf16[16,1408]{1,0:T(8,128)(2,1)S(1)}, bf16[16,1408]{1,0:T(8,128)(2,1)S(1)}, u32[]{:S(2)}, u32[]{:S(2)}) collective-permute-start(bf16[16,1408]{1,0:T(8,128)(2,1)S(1)} %get-tuple-element.15), channel_id=1, source_target_pairs={{0,2},{1,3},{2,0},{3,1},{4,6},{5,7},{6,4},{7,5},{8,10},{9,11},{10,... | collective-permute-start | bytes 135176 | tf_op jit(solution)/shard_map/ppermute | solution.py:541
  19.9 2.6 %collective-permute-done.1.near_ref = bf16[16,1408]{1,0:T(8,128)(2,1)S(1)} collective-permute-done((bf16[16,1408]{1,0:T(8,128)(2,1)S(1)}, bf16[16,1408]{1,0:T(8,128)(2,1)S(1)}, u32[]{:S(2)}, u32[]{:S(2)}) %collective-permute-start.1) | collective-permute-done | bytes 45088 | tf_op jit(solution)/shard_map/ppermute | solution.py:541
  22.5 0.0 collective-permute-done.5.refs_3_
  22.5 0.0 collective-permute-done.6.refs_4_
  22.6 0.0 collective-permute-done.7.refs_5_
  22.6 0.0 copy-done
  22.6 0.0 copy-done.1
  22.6 0.0 copy-done.2
  22.6 0.0 copy-done.3
  22.6 1.4 %spectrum.1 = f32[16,4096]{1,0:T(8,128)} custom-call(bf16[16,1408]{1,0:T(8,128)(2,1)S(1)} %get-tuple-element.14.own_ref, bf16[16,1408]{1,0:T(8,128)(2,1)S(1)} %collective-permute-done.1.near_ref, bf16[2,16,1408]{2,1,0:T(8,128)(2,1)S(1)} %collective-permute-done.2.refs_0_, bf16[2,16,1408]{2,1,0:T(8,128)(2,1)S(1)} %collective-permute-done.3.refs_1_, ...), custom_call_target="tpu_custom_call" | custom-call | tf_op jit(solution)/shard_map/spectrum/pallas_call | solution.py:551
Async XLA Ops:
  3.0 1.7 %collective-permute-start = (bf16[4,2,16,896]{3,2,1,0:T(8,128)(2,1)S(1)}, bf16[4,2,16,896]{3,2,1,0:T(8,128)(2,1)S(1)}, u32[]{:S(2)}, u32[]{:S(2)}) collective-permute-start(bf16[4,2,16,896]{3,2,1,0:T(8,128)(2,1)S(1)} %get-tuple-element.13), channel_id=1, source_target_pairs={{0,1},{1,0},{2,3},{3,2},{4,5},{5,4},{6,7},{7,6},{8,9},{9,8},{10,11... | collective-permute-start | bytes 688136 | tf_op jit(solution)/shard_map/ppermute | solution.py:527
  4.7 17.9 %copy-start = (bf16[128,256]{1,0:T(8,128)(2,1)S(1)}, bf16[128,256]{1,0:T(8,128)(2,1)}, u32[]{:S(2)}) copy-start(bf16[128,256]{1,0:T(8,128)(2,1)} %constant.11.clone.refs_9_) | copy-start | bytes 196612
  4.7 17.9 %copy-start.1 = (f32[64,128]{1,0:T(8,128)S(1)}, f32[64,128]{1,0:T(8,128)}, u32[]{:S(2)}) copy-start(f32[64,128]{1,0:T(8,128)} %constant.10.clone.refs_8_) | copy-start | bytes 98308
  4.7 17.9 %copy-start.2 = (f32[64,128]{1,0:T(8,128)S(1)}, f32[64,128]{1,0:T(8,128)}, u32[]{:S(2)}) copy-start(f32[64,128]{1,0:T(8,128)} %constant.9.clone.refs_7_) | copy-start | bytes 98308
  4.7 17.9 %copy-start.3 = (bf16[128,88]{1,0:T(8,128)(2,1)S(1)}, bf16[128,88]{1,0:T(8,128)(2,1)}, u32[]{:S(2)}) copy-start(bf16[128,88]{1,0:T(8,128)(2,1)} %constant.8.clone.refs_6_) | copy-start | bytes 67588
  4.8 5.9 %collective-permute-start.2 = (bf16[2,16,1408]{2,1,0:T(8,128)(2,1)S(1)}, bf16[2,16,1408]{2,1,0:T(8,128)(2,1)S(1)}, u32[]{:S(2)}, u32[]{:S(2)}) collective-permute-start(bf16[2,16,1408]{2,1,0:T(8,128)(2,1)S(1)} %get-tuple-element.16), channel_id=1, source_target_pairs={{0,4},{1,7},{2,6},{3,5},{4,0},{5,3},{6,2},{7,1},{8,12},{9,15},{10,... | collective-permute-start | bytes 270344 | tf_op jit(solution)/shard_map/ppermute | solution.py:541
  7.8 10.2 %collective-permute-start.3 = (bf16[2,16,1408]{2,1,0:T(8,128)(2,1)S(1)}, bf16[2,16,1408]{2,1,0:T(8,128)(2,1)S(1)}, u32[]{:S(2)}, u32[]{:S(2)}) collective-permute-start(bf16[2,16,1408]{2,1,0:T(8,128)(2,1)S(1)} %get-tuple-element.17), channel_id=1, source_target_pairs={{0,8},{1,11},{2,10},{3,9},{4,12},{5,15},{6,14},{7,13},{8,0},{9,3},... | collective-permute-start | bytes 270344 | tf_op jit(solution)/shard_map/ppermute | solution.py:541
  10.4 8.1 %collective-permute-start.4 = (bf16[2,16,1408]{2,1,0:T(8,128)(2,1)S(1)}, bf16[2,16,1408]{2,1,0:T(8,128)(2,1)S(1)}, u32[]{:S(2)}, u32[]{:S(2)}) collective-permute-start(bf16[2,16,1408]{2,1,0:T(8,128)(2,1)S(1)} %get-tuple-element.18), channel_id=1, source_target_pairs={{0,12},{1,15},{2,14},{3,13},{4,8},{5,11},{6,10},{7,9},{8,4},{9,7},... | collective-permute-start | bytes 270344 | tf_op jit(solution)/shard_map/ppermute | solution.py:541
  10.8 11.8 %collective-permute-start.5 = (bf16[2,16,1408]{2,1,0:T(8,128)(2,1)S(1)}, bf16[2,16,1408]{2,1,0:T(8,128)(2,1)S(1)}, u32[]{:S(2)}, u32[]{:S(2)}) collective-permute-start(bf16[2,16,1408]{2,1,0:T(8,128)(2,1)S(1)} %collective-permute-done.2.refs_0_), channel_id=1, source_target_pairs={{0,1},{1,0},{2,3},{3,2},{4,5},{5,4},{6,7},{7,6},{8,9},{9,8},{10,11... | collective-permute-start | bytes 270344 | tf_op jit(solution)/shard_map/ppermute | solution.py:545
  18.0 4.6 %collective-permute-start.6 = (bf16[2,16,1408]{2,1,0:T(8,128)(2,1)S(1)}, bf16[2,16,1408]{2,1,0:T(8,128)(2,1)S(1)}, u32[]{:S(2)}, u32[]{:S(2)}) collective-permute-start(bf16[2,16,1408]{2,1,0:T(8,128)(2,1)S(1)} %collective-permute-done.3.refs_1_), channel_id=1, source_target_pairs={{0,1},{1,0},{2,3},{3,2},{4,5},{5,4},{6,7},{7,6},{8,9},{9,8},{10,11... | collective-permute-start | bytes 270344 | tf_op jit(solution)/shard_map/ppermute | solution.py:545
  18.5 4.1 %collective-permute-start.7 = (bf16[2,16,1408]{2,1,0:T(8,128)(2,1)S(1)}, bf16[2,16,1408]{2,1,0:T(8,128)(2,1)S(1)}, u32[]{:S(2)}, u32[]{:S(2)}) collective-permute-start(bf16[2,16,1408]{2,1,0:T(8,128)(2,1)S(1)} %collective-permute-done.4.refs_2_), channel_id=1, source_target_pairs={{0,1},{1,0},{2,3},{3,2},{4,5},{5,4},{6,7},{7,6},{8,9},{9,8},{10,11... | collective-permute-start | bytes 270344 | tf_op jit(solution)/shard_map/ppermute | solution.py:545
  18.5 4.1 %collective-permute-start.1 = (bf16[16,1408]{1,0:T(8,128)(2,1)S(1)}, bf16[16,1408]{1,0:T(8,128)(2,1)S(1)}, u32[]{:S(2)}, u32[]{:S(2)}) collective-permute-start(bf16[16,1408]{1,0:T(8,128)(2,1)S(1)} %get-tuple-element.15), channel_id=1, source_target_pairs={{0,2},{1,3},{2,0},{3,1},{4,6},{5,7},{6,4},{7,5},{8,10},{9,11},{10,... | collective-permute-start | bytes 135176 | tf_op jit(solution)/shard_map/ppermute | solution.py:541

commit v4 on v3

--- a/solution.py
+++ b/solution.py
@@ -176,7 +176,8 @@
     for load in loads:
         load.start()
 
-    final_ref[...] = jnp.zeros(final_ref.shape, final_ref.dtype)
+    for edge in (slice(0, LANES), slice(margin + window, final_ref.shape[0])):
+        final_ref[edge] = jnp.zeros((edge.stop - edge.start, dmax), final_ref.dtype)
     lane = lax.broadcasted_iota(jnp.int32, (8, LANES), 1)
 
     def narrow(numbers):
@@ -383,7 +384,7 @@
             ].astype(jnp.float32)
     lines = halves // 2
     lane = lax.broadcasted_iota(jnp.int32, (lines, LANES), 1)
-    group = 4
+    group = 8
     stores = []
 
     def first_stage(start):

time: 24.1 us -> 24.1 us (level)
  no operation moved by 1% of the time
where the time goes in v4:
time: 24.1 us; the launch traced here: 23.9 us
  waiting for transfers between devices  10.3 us (43%)
  starting transfers between devices  9.11 us (38%)
  Pallas kernels  4.44 us (18%)
    ppermute x4, waiting for transfers between devices, slice_plan(): arrived.append(on_chip(lax.ppermute(message, 'sub', route)))  9.18 us
    ppermute x4, starting transfers between devices, slice_plan(): arrived.append(on_chip(lax.ppermute(message, 'sub', route)))  7.05 us
    pallas_call x1, Pallas kernels, slice_plan(): pl.pallas_call(functools.partial(tree_kernel, owners, margin), out_shape=...  3.02 us
    ppermute x3, starting transfers between devices, slice_plan(): relayed.append(on_chip(lax.ppermute(arrived[ring - 1], 'sub', beside)))  1.5 us
    pallas_call x1, Pallas kernels, slice_plan(): pl.pallas_call(functools.partial(spectrum_kernel, rings, 1.0 / (SAMPLES *...  1.33 us
    ppermute x1, waiting for transfers between devices, slice_plan(): got = on_chip(lax.ppermute(send, 'sub', beside))  1.12 us
    ppermute x1, starting transfers between devices, slice_plan(): got = on_chip(lax.ppermute(send, 'sub', beside))  0.56 us
  transfers between devices with their start and end apart: 8, of which 4 were waited for; matrix products, arithmetic and copies ran while one was open for 0% of the time, Pallas kernels for 0%

profile of v4, /device:TPU:0, one launch (start us, length us, event | category | flops | bytes accessed | tf_op | source)
XLA Modules:
  0.0 23.9 jit_solution(2439016713992133029)
XLA Ops:
  0.0 3.0 %tree.1 = (bf16[256,896]{1,0:T(8,128)(2,1)S(1)}, bf16[4,2,16,896]{3,2,1,0:T(8,128)(2,1)S(1)}) custom-call(bf16[528,512]{1,0:T(8,128)(2,1)} %samples_at.1, s32[1,512]{1,0:T(1,128)} %bitcast.1, s32[9,3,256]{2,1,0:T(4,128)} %table_at.1), custom_call_target="tpu_custom_call" | custom-call | tf_op jit(solution)/shard_map/tree/pallas_call | solution.py:509
  3.0 0.6 %collective-permute-start = (bf16[4,2,16,896]{3,2,1,0:T(8,128)(2,1)S(1)}, bf16[4,2,16,896]{3,2,1,0:T(8,128)(2,1)S(1)}, u32[]{:S(2)}, u32[]{:S(2)}) collective-permute-start(bf16[4,2,16,896]{3,2,1,0:T(8,128)(2,1)S(1)} %get-tuple-element.13), channel_id=1, source_target_pairs={{0,1},{1,0},{2,3},{3,2},{4,5},{5,4},{6,7},{7,6},{8,9},{9,8},{10,11... | collective-permute-start | bytes 688136 | tf_op jit(solution)/shard_map/ppermute | solution.py:528
  3.6 1.1 %collective-permute-done.got_ref = bf16[4,2,16,896]{3,2,1,0:T(8,128)(2,1)S(1)} collective-permute-done((bf16[4,2,16,896]{3,2,1,0:T(8,128)(2,1)S(1)}, bf16[4,2,16,896]{3,2,1,0:T(8,128)(2,1)S(1)}, u32[]{:S(2)}, u32[]{:S(2)}) %collective-permute-start) | collective-permute-done | bytes 229408 | tf_op jit(solution)/shard_map/ppermute | solution.py:528
  4.7 0.0 copy-start
  4.7 0.0 copy-start.1
  4.7 0.0 copy-start.2
  4.7 0.0 copy-start.3
  4.7 0.1 pair.1
  4.8 3.0 %collective-permute-start.2 = (bf16[2,16,1408]{2,1,0:T(8,128)(2,1)S(1)}, bf16[2,16,1408]{2,1,0:T(8,128)(2,1)S(1)}, u32[]{:S(2)}, u32[]{:S(2)}) collective-permute-start(bf16[2,16,1408]{2,1,0:T(8,128)(2,1)S(1)} %get-tuple-element.16), channel_id=1, source_target_pairs={{0,4},{1,7},{2,6},{3,5},{4,0},{5,3},{6,2},{7,1},{8,12},{9,15},{10,... | collective-permute-start | bytes 270344 | tf_op jit(solution)/shard_map/ppermute | solution.py:542
  7.8 2.6 %collective-permute-start.3 = (bf16[2,16,1408]{2,1,0:T(8,128)(2,1)S(1)}, bf16[2,16,1408]{2,1,0:T(8,128)(2,1)S(1)}, u32[]{:S(2)}, u32[]{:S(2)}) collective-permute-start(bf16[2,16,1408]{2,1,0:T(8,128)(2,1)S(1)} %get-tuple-element.17), channel_id=1, source_target_pairs={{0,8},{1,11},{2,10},{3,9},{4,12},{5,15},{6,14},{7,13},{8,0},{9,3},... | collective-permute-start | bytes 270344 | tf_op jit(solution)/shard_map/ppermute | solution.py:542
  10.4 0.0 collective-permute-start.4
  10.4 0.3 %collective-permute-done.2.refs_0_ = bf16[2,16,1408]{2,1,0:T(8,128)(2,1)S(1)} collective-permute-done((bf16[2,16,1408]{2,1,0:T(8,128)(2,1)S(1)}, bf16[2,16,1408]{2,1,0:T(8,128)(2,1)S(1)}, u32[]{:S(2)}, u32[]{:S(2)}) %collective-permute-start.2) | collective-permute-done | bytes 90144 | tf_op jit(solution)/shard_map/ppermute | solution.py:542
  10.8 1.0 %collective-permute-start.5 = (bf16[2,16,1408]{2,1,0:T(8,128)(2,1)S(1)}, bf16[2,16,1408]{2,1,0:T(8,128)(2,1)S(1)}, u32[]{:S(2)}, u32[]{:S(2)}) collective-permute-start(bf16[2,16,1408]{2,1,0:T(8,128)(2,1)S(1)} %collective-permute-done.2.refs_0_), channel_id=1, source_target_pairs={{0,1},{1,0},{2,3},{3,2},{4,5},{5,4},{6,7},{7,6},{8,9},{9,8},{10,11... | collective-permute-start | bytes 270344 | tf_op jit(solution)/shard_map/ppermute | solution.py:546
  11.7 6.2 %collective-permute-done.3.refs_1_ = bf16[2,16,1408]{2,1,0:T(8,128)(2,1)S(1)} collective-permute-done((bf16[2,16,1408]{2,1,0:T(8,128)(2,1)S(1)}, bf16[2,16,1408]{2,1,0:T(8,128)(2,1)S(1)}, u32[]{:S(2)}, u32[]{:S(2)}) %collective-permute-start.3) | collective-permute-done | bytes 90144 | tf_op jit(solution)/shard_map/ppermute | solution.py:542
  18.0 0.5 %collective-permute-start.6 = (bf16[2,16,1408]{2,1,0:T(8,128)(2,1)S(1)}, bf16[2,16,1408]{2,1,0:T(8,128)(2,1)S(1)}, u32[]{:S(2)}, u32[]{:S(2)}) collective-permute-start(bf16[2,16,1408]{2,1,0:T(8,128)(2,1)S(1)} %collective-permute-done.3.refs_1_), channel_id=1, source_target_pairs={{0,1},{1,0},{2,3},{3,2},{4,5},{5,4},{6,7},{7,6},{8,9},{9,8},{10,11... | collective-permute-start | bytes 270344 | tf_op jit(solution)/shard_map/ppermute | solution.py:546
  18.5 0.0 collective-permute-done.4.refs_2_
  18.5 0.0 collective-permute-start.7
  18.5 1.5 %collective-permute-start.1 = (bf16[16,1408]{1,0:T(8,128)(2,1)S(1)}, bf16[16,1408]{1,0:T(8,128)(2,1)S(1)}, u32[]{:S(2)}, u32[]{:S(2)}) collective-permute-start(bf16[16,1408]{1,0:T(8,128)(2,1)S(1)} %get-tuple-element.15), channel_id=1, source_target_pairs={{0,2},{1,3},{2,0},{3,1},{4,6},{5,7},{6,4},{7,5},{8,10},{9,11},{10,... | collective-permute-start | bytes 135176 | tf_op jit(solution)/shard_map/ppermute | solution.py:542
  19.9 2.6 %collective-permute-done.1.near_ref = bf16[16,1408]{1,0:T(8,128)(2,1)S(1)} collective-permute-done((bf16[16,1408]{1,0:T(8,128)(2,1)S(1)}, bf16[16,1408]{1,0:T(8,128)(2,1)S(1)}, u32[]{:S(2)}, u32[]{:S(2)}) %collective-permute-start.1) | collective-permute-done | bytes 45088 | tf_op jit(solution)/shard_map/ppermute | solution.py:542
  22.5 0.0 collective-permute-done.5.refs_3_
  22.5 0.0 collective-permute-done.6.refs_4_
  22.6 0.0 collective-permute-done.7.refs_5_
  22.6 0.0 copy-done
  22.6 0.0 copy-done.1
  22.6 0.0 copy-done.2
  22.6 0.0 copy-done.3
  22.6 1.3 %spectrum.1 = f32[16,4096]{1,0:T(8,128)} custom-call(bf16[16,1408]{1,0:T(8,128)(2,1)S(1)} %get-tuple-element.14.own_ref, bf16[16,1408]{1,0:T(8,128)(2,1)S(1)} %collective-permute-done.1.near_ref, bf16[2,16,1408]{2,1,0:T(8,128)(2,1)S(1)} %collective-permute-done.2.refs_0_, bf16[2,16,1408]{2,1,0:T(8,128)(2,1)S(1)} %collective-permute-done.3.refs_1_, ...), custom_call_target="tpu_custom_call" | custom-call | tf_op jit(solution)/shard_map/spectrum/pallas_call | solution.py:552
Async XLA Ops:
  3.0 1.7 %collective-permute-start = (bf16[4,2,16,896]{3,2,1,0:T(8,128)(2,1)S(1)}, bf16[4,2,16,896]{3,2,1,0:T(8,128)(2,1)S(1)}, u32[]{:S(2)}, u32[]{:S(2)}) collective-permute-start(bf16[4,2,16,896]{3,2,1,0:T(8,128)(2,1)S(1)} %get-tuple-element.13), channel_id=1, source_target_pairs={{0,1},{1,0},{2,3},{3,2},{4,5},{5,4},{6,7},{7,6},{8,9},{9,8},{10,11... | collective-permute-start | bytes 688136 | tf_op jit(solution)/shard_map/ppermute | solution.py:528
  4.7 17.9 %copy-start = (bf16[128,256]{1,0:T(8,128)(2,1)S(1)}, bf16[128,256]{1,0:T(8,128)(2,1)}, u32[]{:S(2)}) copy-start(bf16[128,256]{1,0:T(8,128)(2,1)} %constant.11.clone.refs_9_) | copy-start | bytes 196612
  4.7 17.9 %copy-start.1 = (f32[64,128]{1,0:T(8,128)S(1)}, f32[64,128]{1,0:T(8,128)}, u32[]{:S(2)}) copy-start(f32[64,128]{1,0:T(8,128)} %constant.10.clone.refs_8_) | copy-start | bytes 98308
  4.7 17.9 %copy-start.2 = (f32[64,128]{1,0:T(8,128)S(1)}, f32[64,128]{1,0:T(8,128)}, u32[]{:S(2)}) copy-start(f32[64,128]{1,0:T(8,128)} %constant.9.clone.refs_7_) | copy-start | bytes 98308
  4.7 17.9 %copy-start.3 = (bf16[128,88]{1,0:T(8,128)(2,1)S(1)}, bf16[128,88]{1,0:T(8,128)(2,1)}, u32[]{:S(2)}) copy-start(bf16[128,88]{1,0:T(8,128)(2,1)} %constant.8.clone.refs_6_) | copy-start | bytes 67588
  4.8 5.9 %collective-permute-start.2 = (bf16[2,16,1408]{2,1,0:T(8,128)(2,1)S(1)}, bf16[2,16,1408]{2,1,0:T(8,128)(2,1)S(1)}, u32[]{:S(2)}, u32[]{:S(2)}) collective-permute-start(bf16[2,16,1408]{2,1,0:T(8,128)(2,1)S(1)} %get-tuple-element.16), channel_id=1, source_target_pairs={{0,4},{1,7},{2,6},{3,5},{4,0},{5,3},{6,2},{7,1},{8,12},{9,15},{10,... | collective-permute-start | bytes 270344 | tf_op jit(solution)/shard_map/ppermute | solution.py:542
  7.8 10.2 %collective-permute-start.3 = (bf16[2,16,1408]{2,1,0:T(8,128)(2,1)S(1)}, bf16[2,16,1408]{2,1,0:T(8,128)(2,1)S(1)}, u32[]{:S(2)}, u32[]{:S(2)}) collective-permute-start(bf16[2,16,1408]{2,1,0:T(8,128)(2,1)S(1)} %get-tuple-element.17), channel_id=1, source_target_pairs={{0,8},{1,11},{2,10},{3,9},{4,12},{5,15},{6,14},{7,13},{8,0},{9,3},... | collective-permute-start | bytes 270344 | tf_op jit(solution)/shard_map/ppermute | solution.py:542
  10.4 8.1 %collective-permute-start.4 = (bf16[2,16,1408]{2,1,0:T(8,128)(2,1)S(1)}, bf16[2,16,1408]{2,1,0:T(8,128)(2,1)S(1)}, u32[]{:S(2)}, u32[]{:S(2)}) collective-permute-start(bf16[2,16,1408]{2,1,0:T(8,128)(2,1)S(1)} %get-tuple-element.18), channel_id=1, source_target_pairs={{0,12},{1,15},{2,14},{3,13},{4,8},{5,11},{6,10},{7,9},{8,4},{9,7},... | collective-permute-start | bytes 270344 | tf_op jit(solution)/shard_map/ppermute | solution.py:542
  10.8 11.8 %collective-permute-start.5 = (bf16[2,16,1408]{2,1,0:T(8,128)(2,1)S(1)}, bf16[2,16,1408]{2,1,0:T(8,128)(2,1)S(1)}, u32[]{:S(2)}, u32[]{:S(2)}) collective-permute-start(bf16[2,16,1408]{2,1,0:T(8,128)(2,1)S(1)} %collective-permute-done.2.refs_0_), channel_id=1, source_target_pairs={{0,1},{1,0},{2,3},{3,2},{4,5},{5,4},{6,7},{7,6},{8,9},{9,8},{10,11... | collective-permute-start | bytes 270344 | tf_op jit(solution)/shard_map/ppermute | solution.py:546
  18.0 4.6 %collective-permute-start.6 = (bf16[2,16,1408]{2,1,0:T(8,128)(2,1)S(1)}, bf16[2,16,1408]{2,1,0:T(8,128)(2,1)S(1)}, u32[]{:S(2)}, u32[]{:S(2)}) collective-permute-start(bf16[2,16,1408]{2,1,0:T(8,128)(2,1)S(1)} %collective-permute-done.3.refs_1_), channel_id=1, source_target_pairs={{0,1},{1,0},{2,3},{3,2},{4,5},{5,4},{6,7},{7,6},{8,9},{9,8},{10,11... | collective-permute-start | bytes 270344 | tf_op jit(solution)/shard_map/ppermute | solution.py:546
  18.5 4.1 %collective-permute-start.7 = (bf16[2,16,1408]{2,1,0:T(8,128)(2,1)S(1)}, bf16[2,16,1408]{2,1,0:T(8,128)(2,1)S(1)}, u32[]{:S(2)}, u32[]{:S(2)}) collective-permute-start(bf16[2,16,1408]{2,1,0:T(8,128)(2,1)S(1)} %collective-permute-done.4.refs_2_), channel_id=1, source_target_pairs={{0,1},{1,0},{2,3},{3,2},{4,5},{5,4},{6,7},{7,6},{8,9},{9,8},{10,11... | collective-permute-start | bytes 270344 | tf_op jit(solution)/shard_map/ppermute | solution.py:546
  18.5 4.1 %collective-permute-start.1 = (bf16[16,1408]{1,0:T(8,128)(2,1)S(1)}, bf16[16,1408]{1,0:T(8,128)(2,1)S(1)}, u32[]{:S(2)}, u32[]{:S(2)}) collective-permute-start(bf16[16,1408]{1,0:T(8,128)(2,1)S(1)} %get-tuple-element.15), channel_id=1, source_target_pairs={{0,2},{1,3},{2,0},{3,1},{4,6},{5,7},{6,4},{7,5},{8,10},{9,11},{10,... | collective-permute-start | bytes 135176 | tf_op jit(solution)/shard_map/ppermute | solution.py:542
